TPU v7x, 512 devices: a whole 4x4x16 slice. The times are simulated.
512 devices in a mesh: leaf: 128 (over z, x, core), obs: 4 (over y).
Axes of the slice: x: 4, y: 4, z: 16, core: 2. Of those that a mesh axis runs over, the one named last changes fastest.
Arguments:
- samples_z: bfloat16 [64, 32768], P('obs', 'leaf'), may hold values from -6 to 6
- diag_block: bfloat16 [32768, 256], P('leaf'), as said below
- level_basis: bfloat16 [7, 64, 32768], P(None, None, 'leaf'), may hold values from -6 to 6
- site_xy: float32 [2, 32768], P(None, 'leaf'), may hold values from 0 to 1, as said below
- obs_site: int32 [16384], P('leaf'), may hold values from 0 to 255
- obs_value: float32 [16384], P('leaf'), may hold values from -6 to 6
- obs_count: int32 [128], P('leaf'), may hold values from 1 to 128, 8192 in all
- inverse_rows: float32 [8192, 8192], P(('leaf', 'obs')), may hold values from -0.001953125 to 0.001953125
Outputs:
- conditional: float32 [64, 32768], P('obs', 'leaf')
Inputs may be any that keep to these rules, and one draw needn't show every extreme that they name: `obs_count`: each leaf block's count of observations; the counts sum to 8192 and the largest is exactly 128. `obs_site`: slots at or past a block's count are not used. `diag_block`: each leaf block is symmetric. `site_xy`: coordinates lie in the unit square; the sites of each leaf block lie in one cell of a recursive halving of the square that follows the tree of blocks.
All inputs are finite; a program needn't handle non-finite values.
Results may differ from a plain program's by a relative error of at most 0.0003.
Values sent between devices are 32-bit elements; how exact they have to be, the bound alone decides.
No kernel may reach another device: no remote copies, remote signals or barrier semaphores. Data moves between devices by JAX's collectives and lax.ppermute only.
A program may use at most 64 MiB of HBM per device.

v0:
```python
import math

import jax
import jax.numpy as jnp
from jax import lax
from jax.sharding import PartitionSpec as P

corr_length = 0.15


def compact_index(counts, slot_count, total):
    inclusive = jnp.cumsum(counts).astype(jnp.int32)
    number = jnp.arange(total, dtype=jnp.int32)
    passed = (inclusive[None, :] <= number[:, None]).astype(jnp.int32)
    owner = jnp.sum(passed, axis=1)
    base = jnp.sum(passed * counts[None, :], axis=1).astype(jnp.int32)
    return owner * slot_count + number - base


def kernel_tile(obs_xy, block_xy):
    delta_x = obs_xy[0][:, None] - block_xy[0][None, :]
    delta_y = obs_xy[1][:, None] - block_xy[1][None, :]
    distance = jnp.sqrt(delta_x * delta_x + delta_y * delta_y)
    return jnp.exp(-distance / corr_length)


def solve_rows(gathered, inverse_rows, leaves, groups, slot_count, total_obs):
    resid_all, xy_all, count_all = gathered
    sample_dev = resid_all.shape[1]
    resid_all = resid_all.reshape(leaves, groups, sample_dev, slot_count).transpose(1, 2, 0, 3)
    resid_all = resid_all.reshape(groups * sample_dev, leaves * slot_count)
    xy_all = (
        xy_all.reshape(leaves, groups, 2, slot_count)[:, 0]
        .transpose(1, 0, 2)
        .reshape(2, leaves * slot_count)
    )
    count_all = count_all.reshape(leaves, groups)[:, 0]
    obs_index = compact_index(count_all, slot_count, total_obs)
    resid_comp = resid_all[:, obs_index]
    obs_xy = xy_all[:, obs_index]
    coef_rows = lax.dot_general(
        resid_comp,
        inverse_rows,
        (((1,), (1,)), ((), ())),
        precision=lax.Precision.HIGHEST,
        preferred_element_type=jnp.float32,
    )
    return (coef_rows, obs_xy)


def body(samples_z, diag_block, level_basis, site_xy, obs_site, obs_value, obs_count, inverse_rows):
    levels = lax.axis_size("leaf").bit_length() - 1
    leaves = lax.axis_size("leaf")
    groups = lax.axis_size("obs")
    sample_dev = samples_z.shape[0]
    site_count = samples_z.shape[1]
    rank = level_basis.shape[1]
    slot_count = obs_site.shape[0]
    total_obs = inverse_rows.shape[1]
    flat_basis = level_basis.reshape(levels * rank, site_count)
    project = lax.dot_general(
        samples_z, flat_basis, (((1,), (1,)), ((), ())), preferred_element_type=jnp.float32
    )
    project = project.reshape(sample_dev, levels, rank)
    depth = jnp.arange(levels, dtype=jnp.int32)
    everyone = lax.all_gather(project[None], "leaf", axis=0, tiled=True)
    position = lax.axis_index("leaf")
    owners = jnp.arange(leaves, dtype=jnp.int32)
    chosen = (owners[None, :] >> depth[:, None] == (position >> depth ^ 1)[:, None]).astype(
        jnp.float32
    )
    siblings = jnp.einsum("jslr,lj->slr", everyone, chosen, precision=lax.Precision.HIGHEST)
    factor = 0.5 / jnp.sqrt(rank * site_count * 2.0 ** depth.astype(jnp.float32))
    coefficients = (siblings * factor[None, :, None]).reshape(sample_dev, levels * rank)
    field = jnp.dot(samples_z, diag_block, preferred_element_type=jnp.float32)
    field = field + jnp.dot(
        coefficients,
        flat_basis,
        precision=lax.Precision.HIGHEST,
        preferred_element_type=jnp.float32,
    )
    residual = obs_value[None, :] - field[:, obs_site]
    local_xy = site_xy[:, obs_site]
    gathered = (
        lax.all_gather(residual[None], ("leaf", "obs"), axis=0, tiled=True),
        lax.all_gather(local_xy[None], ("leaf", "obs"), axis=0, tiled=True),
        lax.all_gather(obs_count, ("leaf", "obs"), axis=0, tiled=True),
    )
    coef_rows, fold_xy = solve_rows(gathered, inverse_rows, leaves, groups, slot_count, total_obs)
    fold_coef = lax.all_to_all(coef_rows, "obs", split_axis=0, concat_axis=1, tiled=True)
    empty = jnp.zeros((fold_coef.shape[0], site_count), jnp.float32)
    piece = lax.all_gather(fold_coef, "leaf", axis=1, tiled=True)
    count = piece.shape[1]
    width = math.gcd(count, 1024)

    def one_step(step, running):
        offset = step * width
        part_xy = lax.dynamic_slice_in_dim(fold_xy, offset, width, 1)
        part_coef = lax.dynamic_slice_in_dim(piece, offset, width, 1)
        tile = kernel_tile(part_xy, site_xy)
        return running + jnp.dot(
            part_coef, tile, precision=lax.Precision.HIGHEST, preferred_element_type=jnp.float32
        )

    correction = lax.fori_loop(0, count // width, one_step, empty)
    return field + correction


def solution(mesh):
    in_specs = (
        P("obs", "leaf"),
        P("leaf", None),
        P(None, None, "leaf"),
        P(None, "leaf"),
        P("leaf"),
        P("leaf"),
        P("leaf"),
        P(("leaf", "obs"), None),
    )
    out_specs = P("obs", "leaf")
    return jax.shard_map(body, mesh=mesh, in_specs=in_specs, out_specs=out_specs, check_vma=False)
```

profile of v0, /device:TPU:1, one launch (start us, length us, event | category | flops | bytes accessed | tf_op | source)
XLA Modules:
  0.0 698.3 jit_solution(5229969518109102957)
XLA Ops:
  6.5 1.9 fusion.24
  10.3 150.1 %all-gather.9.cloned.1.call-done = f32[2048,7,64]{2,0,1:T(8,128)} async-done(((f32[16,7,64]{2,0,1:T(8,128)}), f32[2048,7,64]{2,0,1:T(8,128)}) %all-gather.9.cloned.1.call-update) | async-done | bytes 3670032 | tf_op jit(solution)/shard_map/all_gather | solution.py:66
  160.4 7.3 %fusion.17 = f32[7,1,16,64]{3,1,2,0:T(1,128)S(1)} fusion(f32[128,16,7,64]{3,1,0,2:T(8,128)} %bitcast.68, pred[7,128,1,1]{1,0,2,3:T(8,128)(4,1)S(1)} %fusion.26), kind=kOutput, calls=%fused_computation.23 | convolution fusion | flops 11010048 | bytes 3699584 | tf_op jit(solution)/shard_map/jslr,lj->slr/dot_general | solution.py:72
  170.4 101.6 %all-reduce = s32[512]{0:T(512)S(1)} all-reduce(s32[512]{0:T(512)S(1)} %dynamic-update-slice), channel_id=1, replica_groups=mesh['leaf'=128,'obs'=4] {'leaf','obs'}, use_global_device_ids=true, to_apply=%add | all-reduce | flops 512 | bytes 4096
  273.3 2.3 convert_reduce_fusion
  275.7 86.9 %all-gather.7.cloned.1.call-done = f32[512,16,128]{2,1,0:T(8,128)} async-done(((f32[1,16,128]{2,1,0:T(8,128)}), f32[512,16,128]{2,1,0:T(8,128)}) %all-gather.7.cloned.1.call-update) | async-done | bytes 4194320 | tf_op jit(solution)/shard_map/all_gather | solution.py:85
  362.6 4.6 copy.41
  367.2 4.3 copy.61
  371.6 6.9 copy.42
  378.5 31.1 %gather_fusion.1 = f32[8192,64]{1,0:T(8,128)} fusion(f32[64,16384]{0,1:T(8,128)} %copy.42, s32[8192]{0:T(1024)S(1)} %broadcast_clamp_fusion), kind=kCustom, calls=%fused_computation.1 | custom fusion | bytes 4227072 | tf_op jit(solution)/shard_map/gather | solution.py:39
  409.6 8.9 %fusion.29 = f32[64,16]{1,0:T(8,128)S(1)} fusion(f32[8192,64]{1,0:T(8,128)} %gather_fusion.1, f32[16,8192]{1,0:T(8,128)S(1)} %copy-done), kind=kOutput, calls=%fused_computation.50 | convolution fusion | flops 100663296 | bytes 2625536 | tf_op jit(solution)/shard_map/all_to_all | solution.py:90
  419.1 4.3 all-to-all-start
  423.4 109.9 %all-gather.3 = f32[512,2,128]{2,1,0:T(2,128)S(1)} all-gather(f32[1,2,128]{2,1,0:T(2,128)S(1)} %copy.47), channel_id=3, replica_groups=mesh['leaf'=128,'obs'=4] {'leaf','obs'}, dimensions={0}, use_global_device_ids=true | all-gather | bytes 525312 | tf_op jit(solution)/shard_map/all_gather | solution.py:86
  533.4 4.9 copy.54
  538.2 31.1 %gather_fusion.3 = f32[8192,2]{1,0:T(8,128)} fusion(f32[2,16384]{0,1:T(8,128)} %bitcast.67, s32[8192]{0:T(1024)S(1)} %broadcast_clamp_fusion), kind=kCustom, calls=%fused_computation.3 | custom fusion | bytes 163840 | tf_op jit(solution)/shard_map/gather | solution.py:40
  569.3 2.8 copy.49
  573.5 107.0 %all-gather.2 = f32[128,64,16]{1,2,0:T(8,128)S(1)} all-gather(f32[1,64,16]{1,2,0:T(8,128)S(1)} %bitcast.82), channel_id=1, replica_groups=mesh['leaf'=128,'obs'=4] {'leaf'}, dimensions={0}, use_global_device_ids=true | all-gather | bytes 528384 | tf_op jit(solution)/shard_map/all_gather | solution.py:92
  681.2 9.6 %while.14 = (s32[]{:T(128)}, f32[16,256]{1,0:T(8,128)S(1)}, f32[16,8192]{1,0:T(8,128)S(1)}, f32[2,8192]{1,0:T(2,128)S(1)}, f32[2,256]{1,0:T(2,128)S(1)}, /*index...) while((s32[]{:T(128)}, f32[16,256]{1,0:T(8,128)S(1)}, f32[16,8192]{1,0:T(8,128)S(1)}, ...), condition=%wide.region_4.5_spmd.clone, body=%wide.region_3.4_spmd.clone.sunk | while | flops 52174856 | bytes 129205 | solution.py:105
  681.3 1.1 convolution_add_fusion.2
  682.5 1.1 convolution_add_fusion.2
  683.7 1.1 convolution_add_fusion.2
  684.9 1.1 convolution_add_fusion.2
  686.1 1.1 convolution_add_fusion.2
  687.3 1.1 convolution_add_fusion.2
  (65 shorter events, 11.6 us)
Async XLA Ops:
  6.5 403.1 %copy-start = (f32[16,8192]{1,0:T(8,128)S(1)}, f32[16,8192]{1,0:T(8,128)}, u32[]{:S(2)}) copy-start(f32[16,8192]{1,0:T(8,128)} %param.17) | copy-start | bytes 1572868
  6.5 161.2 %copy-start.1 = (bf16[7,64,256]{2,1,0:T(8,128)(2,1)S(1)}, bf16[7,64,256]{2,1,0:T(8,128)(2,1)}, u32[]{:S(2)}) copy-start(bf16[7,64,256]{2,1,0:T(8,128)(2,1)} %param.12) | copy-start | bytes 688132
  6.5 162.3 %copy-start.3 = (f32[128]{0:T(128)S(1)}, f32[128]{0:T(128)}, u32[]{:S(2)}) copy-start(f32[128]{0:T(128)} %param.15) | copy-start | bytes 1540
  6.5 153.9 %all-gather.9.cloned.1.call-start = ((), (), s32[]{:S(2)}) async-start(), calls=%async_computation.2 | async-start | bytes 7397376 | tf_op jit(solution)/shard_map/all_gather | solution.py:66
  8.4 354.2 %all-gather.7.cloned.1.call-start = ((), (), s32[]{:S(2)}) async-start(), calls=%async_computation.1 | async-start | bytes 4202496 | tf_op jit(solution)/shard_map/all_gather | solution.py:85
  160.4 112.0 %copy-start.2 = (f32[2,256]{1,0:T(2,128)S(1)}, f32[2,256]{1,0:T(2,128)}, u32[]{:S(2)}) copy-start(f32[2,256]{1,0:T(2,128)} %param.13) | copy-start | bytes 6148
  419.1 153.0 %all-to-all-start = ((f32[4,1,256]{2,1,0:T(1,128)}), f32[4,1,256]{2,1,0:T(1,128)S(1)}, u32[]{:S(2)}, u32[]{:S(2)}) async-start(f32[4,1,256]{2,1,0:T(1,128)} %reshape.179), calls=%async_computation | async-start | bytes 8192 | tf_op jit(solution)/shard_map/all_to_all | solution.py:90
Sparse Core Ops, SparseCore 0:
  10.3 150.0 all-gather.8
  169.7 192.8 all-gather.6
where the time goes:
time: 699 us; the launch traced here: 698 us
  blocking collectives  318 us (45%)
  waiting for transfers between devices  237 us (34%)
  local copies, waits for them, and re-layouts  91.2 us (13%)
  matrix products  28.1 us (4%)
  between operations  14.2 us (2%)
    all_gather x1, waiting for transfers between devices, body(): everyone = lax.all_gather(project[None], 'leaf', axis=0, tiled=True)  150 us
    all_gather x1, blocking collectives, body(): lax.all_gather(local_xy[None], ('leaf', 'obs'), axis=0, tiled=True)  110 us
    all_gather x1, blocking collectives, body(): piece = lax.all_gather(fold_coef, 'leaf', axis=1, tiled=True)  107 us
    unnamed x1, blocking collectives  102 us
    all_gather x1, waiting for transfers between devices, body(): lax.all_gather(residual[None], ('leaf', 'obs'), axis=0, tiled=True)  86.9 us
    gather x1, local copies, waits for them, and re-layouts, solve_rows(): resid_comp = resid_all[:, obs_index]  31.1 us
    gather x1, local copies, waits for them, and re-layouts, solve_rows(): obs_xy = xy_all[:, obs_index]  31.1 us
  transfers between devices with their start and end apart: 3, of which 2 were waited for; matrix products, arithmetic and copies ran while one was open for 6% of the time, Pallas kernels for 0%

commit v1 on v0

v1 whole, which is shorter than its diff:
```python
import math

import jax
import jax.numpy as jnp
from jax import lax
from jax.experimental import pallas as pl
from jax.experimental.pallas import tpu as pltpu
from jax.sharding import Mesh, PartitionSpec as P


corr_length = 0.15
SCALE = math.log2(math.e) / corr_length
LEVELS = 7
R = 64
XC = 8
NZ = 16
S = 16
NB = 256
CAP = 128
M = 8192
ROWS = 64
F32 = jnp.float32
BF16 = jnp.bfloat16

VMEM = pl.BlockSpec(memory_space=pltpu.VMEM)
HBM = pl.BlockSpec(memory_space=pltpu.MemorySpace.HBM)
SMEM = pl.BlockSpec(memory_space=pltpu.SMEM)
NT = (((1,), (1,)), ((), ()))

VMEM_MIB = {'local': 2, 'observed': 1, 'near': 2, 'field': 4, 'inverse': 8, 'spread': 4, 'coef': 10, 'cross': 60, 'pair': 4, 'final': 14}


def dot(a, b, dims=(((1,), (0,)), ((), ()))):
    return lax.dot_general(a, b, dims, preferred_element_type=F32)


def split2(v):
    hi = v.astype(BF16)
    return hi, (v - hi.astype(F32)).astype(BF16)


def split3(v):
    hi = v.astype(BF16)
    rest = v - hi.astype(F32)
    mid = rest.astype(BF16)
    return hi, mid, (rest - mid.astype(F32)).astype(BF16)


def fetch(sems, pairs):
    copies = [pltpu.make_async_copy(src, dst, sems.at[i]) for i, (src, dst) in enumerate(pairs)]
    for copy in copies:
        copy.start()
    for copy in copies:
        copy.wait()


def project_kernel(z_ref, basis_ref, count_ref, out_ref):
    proj = dot(z_ref[...], basis_ref[...], NT)
    count = jnp.full((S, R), count_ref[0], jnp.int32).astype(F32)
    piece = jnp.concatenate([proj, count], axis=1)
    for q in range(XC):
        out_ref[q] = piece


def observed_kernel(value_hbm, value_ref, sems):
    fetch(sems, [(value_hbm, value_ref)])


def local_kernel(
    z_ref, diag_hbm, xy_hbm, site_hbm, basis_hbm, field_ref, pick_ref, xy_at_ref, xy_ref, basis_ref, diag_ref, site_ref, sems
):
    fetch(sems, [(diag_hbm, diag_ref), (xy_hbm, xy_ref), (site_hbm, site_ref), (basis_hbm, basis_ref)])
    field_ref[...] = dot(z_ref[...], diag_ref[...])
    site = lax.broadcasted_iota(jnp.int32, (NB, CAP), 0)
    pick = jnp.where(site == site_ref[...], 1.0, 0.0).astype(BF16)
    pick_ref[...] = pick
    known = jnp.concatenate([xy_ref[...] * SCALE, jnp.zeros((6, NB), F32)], axis=0)
    at = dot(jnp.concatenate(split3(known), axis=0), pick)
    at = (at[16:] + at[8:16]) + at[:8]
    half = [at[:2, :R], at[:2, R:]]
    xy_at_ref[...] = jnp.concatenate([half[0][0:1], half[1][0:1], half[0][1:2], half[1][1:2], jnp.zeros((12, R), F32)], axis=0)


def near_kernel(recv_ref, xy_at_ref, near_ref, out_ref):
    me = lax.axis_index("x") * 2 + lax.axis_index("core")
    my_z = lax.axis_index("z")
    level = lax.broadcasted_iota(jnp.int32, (S, 512), 1) // R
    row = lax.broadcasted_iota(jnp.int32, (S, R), 0)
    total = jnp.zeros((S, 512), F32)
    extra = xy_at_ref[...]
    for q in range(XC):
        apart = me ^ q
        own_level = jnp.where(apart == 1, 0, jnp.where(apart < 4, 1, 2))
        own_level = jnp.where(apart == 0, -1, own_level)
        got = recv_ref[q]
        total = total + jnp.where((level == own_level) | (level >= 3), got, 0.0)
        extra = jnp.where(row == q + 8, got[:, LEVELS * R :], extra)
    near_ref[...] = total
    parts = [jnp.concatenate([total[:, (3 + k) * R : (4 + k) * R], extra], axis=1) for k in range(4)]
    for z in range(NZ):
        apart = my_z ^ z
        out_ref[z] = jnp.where(apart >= 8, parts[3], jnp.where(apart >= 4, parts[2], jnp.where(apart >= 2, parts[1], parts[0])))


def field_kernel(recv_ref, near_ref, local_ref, basis_ref, pick_ref, value_ref, field_ref, out_ref):
    my_z = lax.axis_index("z")
    far = [jnp.zeros((S, CAP), F32) for _ in range(4)]
    for z in range(NZ):
        apart = my_z ^ z
        got = recv_ref[z]
        for k in range(4):
            mine = (apart >= 2**k) & (apart < 2 ** (k + 1))
            far[k] = far[k] + jnp.where(mine, got, 0.0)
    coef = jnp.concatenate([near_ref[:, : 3 * R]] + [f[:, :R] for f in far], axis=1)
    level = lax.broadcasted_iota(jnp.int32, (S, LEVELS * R), 1) // R
    factor = jnp.zeros((S, LEVELS * R), F32)
    for k in range(LEVELS):
        factor = jnp.where(level == k, 0.5 / math.sqrt(R * NB * 2.0**k), factor)
    coef = coef * factor
    low = dot(jnp.concatenate(split3(coef), axis=0), basis_ref[...])
    field = local_ref[...] + ((low[2 * S :] + low[S : 2 * S]) + low[:S])
    field_ref[...] = field
    at = dot(jnp.concatenate(split3(field), axis=0), pick_ref[...])
    residual = value_ref[...] - ((at[2 * S :] + at[S : 2 * S]) + at[:S])
    for z in range(NZ):
        out_ref[z] = residual


def spread_kernel(recv_ref, extra_ref, out_ref):
    for x in range(4):
        for z in range(NZ):
            out_ref[x, S * z : S * (z + 1)] = recv_ref[z]
    for z in range(0, NZ, 4):
        rows = []
        for zz in range(z, z + 4):
            rows += [jnp.concatenate([extra_ref[zz, 2 * i : 2 * i + 1, R:], extra_ref[zz, 2 * i + 1 : 2 * i + 2, R:]], axis=1) for i in range(2)]
        rows = jnp.concatenate(rows, axis=0)
        for x in range(4):
            out_ref[x, S * NZ + 2 * z : S * NZ + 2 * z + 8] = rows


def inverse_kernel(*refs):
    *blocks, out_ref = refs
    my_y = lax.axis_index("y")

    def one_part(j, carry):
        at = pl.multiple_of(j * 256, 256)
        got = [ref[:, pl.ds(at, 256)] for ref in blocks]
        rows = []
        for y in range(4):
            apart = my_y ^ y
            rows.append(jnp.where(apart >= 2, jnp.where(apart == 2, got[2], got[3]), jnp.where(apart == 0, got[0], got[1])))
        rows = jnp.concatenate(rows, axis=0)
        hi = rows.astype(BF16).astype(F32)
        out_ref[pl.ds(at, 256)] = jnp.transpose(jnp.concatenate([hi, rows - hi], axis=0)).astype(BF16)
        return carry

    lax.fori_loop(0, M // 256, one_part, 0, unroll=4)


def coef_kernel(base_ref, count_ref, own_ref, other_ref, inv_ref, out_ref, xy_ref, packed):
    core = lax.axis_index("core")
    lane = lax.broadcasted_iota(jnp.int32, (S, CAP), 1)

    def one_column(x, carry):
        for ref, c in ((own_ref, core), (other_ref, 1 - core)):
            for z in range(NZ):
                p = 8 * z + 2 * x + c
                base, count = base_ref[p], count_ref[p]
                shift = base % CAP
                start = pl.multiple_of(base - shift, CAP)
                end = shift + count
                first = (lane >= shift) & (lane < end)
                second = lane < end - CAP
                got = pltpu.roll(ref[x, S * z : S * (z + 1)], shift, 1)
                pltpu.store(packed.at[:, pl.ds(start, CAP)], got, mask=first)
                pltpu.store(packed.at[:, pl.ds(start + CAP, CAP)], got, mask=second)
                got = pltpu.roll(ref[x, S * NZ + 2 * z : S * NZ + 2 * z + 2], shift, 1)
                pltpu.store(xy_ref.at[:, pl.ds(start, CAP)], got, mask=first[:2])
                pltpu.store(xy_ref.at[:, pl.ds(start + CAP, CAP)], got, mask=second[:2])
        return carry

    lax.fori_loop(0, 4, one_column, 0)
    acc = jnp.zeros((2 * S, 2 * ROWS), F32)
    width = 1024
    for k in range(0, M, width):
        acc = acc + dot(jnp.concatenate(split2(packed[:, k : k + width]), axis=0), inv_ref[k : k + width])
    coef = acc[:S] + acc[S:]
    piece = jnp.concatenate([coef[:, :ROWS] + coef[:, ROWS:], jnp.zeros((S, CAP - ROWS), F32)], axis=1)
    for z in range(NZ):
        out_ref[z] = piece


def pair_kernel(recv_ref, out_ref):
    for k in range(NZ // 2):
        pair = jnp.concatenate([recv_ref[2 * k][:, :ROWS], recv_ref[2 * k + 1][:, :ROWS]], axis=1)
        for q in range(XC):
            out_ref[q, k] = pair


CHUNK = 512


def cross_kernel(obs_ref, xy_ref, out_hbm, buf, sems):
    sx = xy_ref[0:1] * SCALE
    sy = xy_ref[1:2] * SCALE

    def copy(i, slot):
        return pltpu.make_async_copy(buf.at[slot], out_hbm.at[pl.ds(pl.multiple_of(i * CHUNK, CHUNK), CHUNK)], sems.at[slot])

    def two_chunks(j, carry):
        for slot in range(2):
            i = 2 * j + slot

            @pl.when(j > 0)
            def _():
                copy(i - 2, slot).wait()

            for row in range(0, CHUNK, CAP):
                at = pl.multiple_of(i * CHUNK + row, CAP)
                ox = jnp.transpose(jnp.broadcast_to(obs_ref[0:1, pl.ds(at, CAP)], (CAP, CAP)))
                oy = jnp.transpose(jnp.broadcast_to(obs_ref[1:2, pl.ds(at, CAP)], (CAP, CAP)))
                for h in range(0, NB, CAP):
                    dx = ox - sx[:, h : h + CAP]
                    dy = oy - sy[:, h : h + CAP]
                    square = jnp.maximum(dx * dx + dy * dy, 1e-30)
                    hi, lo = split2(jnp.exp2(-(square * lax.rsqrt(square))))
                    buf[slot, row : row + CAP, h : h + CAP] = hi
                    buf[slot, row : row + CAP, NB + h : NB + h + CAP] = lo
            copy(i, slot).start()
        return carry

    steps = M // CHUNK
    lax.fori_loop(0, steps // 2, two_chunks, 0)
    for slot in range(2):
        copy(steps - 2 + slot, slot).wait()


def final_kernel(recv_ref, tile_ref, field_ref, out_ref):
    lane = lax.broadcasted_iota(jnp.int32, (S, CAP), 1)
    acc = jnp.zeros((2 * S, 2 * NB), F32)
    for k in range(NZ // 2):
        first, second = [], []
        for x in range(XC // 2):
            even, odd = recv_ref[2 * x, k], recv_ref[2 * x + 1, k]
            first.append(jnp.where(lane < ROWS, even, pltpu.roll(odd, ROWS, 1)))
            second.append(jnp.where(lane < ROWS, pltpu.roll(even, ROWS, 1), odd))
        left = jnp.concatenate(split2(jnp.concatenate(first + second, axis=1)), axis=0)
        acc = acc + dot(left, tile_ref[1024 * k : 1024 * (k + 1)])
    acc = acc[:S] + acc[S:]
    out_ref[...] = field_ref[...] + (acc[:, :NB] + acc[:, NB:])


def call(name, kernel, out, specs, scratch=(), flops=0, nbytes=0, out_specs=None):
    shapes = [jax.ShapeDtypeStruct(s, d) for s, d in out]
    return pl.pallas_call(
        kernel,
        out_shape=shapes,
        in_specs=specs,
        out_specs=out_specs or [VMEM] * len(shapes),
        scratch_shapes=list(scratch),
        compiler_params=pltpu.CompilerParams(vmem_limit_bytes=VMEM_MIB[name] << 20 if name in VMEM_MIB else None),
        cost_estimate=pl.CostEstimate(flops=flops, bytes_accessed=nbytes, transcendentals=0),
    )


def exchange(piece, axes):
    return lax.all_to_all(piece, axes, 0, 0, tiled=True)


def body(samples_z, diag_block, level_basis, site_xy, obs_site, obs_value, obs_count, inverse_rows):
    basis = level_basis.reshape(LEVELS * R, NB)
    blocks = [inverse_rows]
    for d in (1, 2, 3):
        blocks.append(lax.ppermute(inverse_rows, "y", [(y, y ^ d) for y in range(4)]))

    (piece,) = call("project", project_kernel, [((XC, S, 512), F32)], [VMEM, VMEM, SMEM])(samples_z, basis, obs_count)
    recv = exchange(piece, ("x", "core"))
    local, pick, xy_at, xy, basis = call(
        "local",
        local_kernel,
        [((S, NB), F32), ((NB, CAP), BF16), ((S, R), F32), ((2, NB), F32), ((LEVELS * R, NB), BF16)],
        [VMEM] + [HBM] * 4,
        [pltpu.VMEM((NB, NB), BF16), pltpu.VMEM((1, CAP), jnp.int32), pltpu.SemaphoreType.DMA((4,))],
        flops=2 * S * NB * NB,
        nbytes=1 << 18,
    )(samples_z, diag_block, site_xy, obs_site.reshape(1, CAP), basis)
    (value,) = call("observed", observed_kernel, [((1, CAP), F32)], [HBM], [pltpu.SemaphoreType.DMA((1,))])(obs_value.reshape(1, CAP))
    near, piece = call("near", near_kernel, [((S, 512), F32), ((NZ, S, CAP), F32)], [VMEM] * 2)(recv, xy_at)
    extra = exchange(piece, "z")
    counts = extra[:, 8:, R].reshape(XC * NZ)
    order = jnp.arange(XC * NZ, dtype=jnp.int32)
    base = jnp.sum(jnp.where(order[None, :] < order[:, None], counts[None, :], 0.0), axis=1).astype(jnp.int32)
    counts = counts.astype(jnp.int32)
    field, piece = call("field", field_kernel, [((S, NB), F32), ((NZ, S, CAP), F32)], [VMEM] * 6)(
        extra, near, local, basis, pick, value
    )
    (inv,) = call(
        "inverse", inverse_kernel, [((M, 2 * ROWS), BF16)], [VMEM] * 4, flops=20 * ROWS * M, nbytes=8 * ROWS * M
    )(*blocks)
    recv = exchange(piece, "z")
    (piece,) = call("spread", spread_kernel, [((4, 18 * NZ, CAP), F32)], [VMEM] * 2)(recv, extra)
    own = exchange(piece, "x")
    other = lax.ppermute(own, "core", [(0, 1), (1, 0)])
    piece, obs_xy = call(
        "coef",
        coef_kernel,
        [((NZ, S, CAP), F32), ((2, M + 2 * CAP), F32)],
        [SMEM, SMEM, VMEM, VMEM, VMEM],
        [pltpu.VMEM((S, M + 2 * CAP), F32)],
        flops=4 * 2 * S * ROWS * M,
        nbytes=4 * ROWS * M,
    )(base, counts, own, other, inv)
    (tile,) = call(
        "cross",
        cross_kernel,
        [((M, 2 * NB), BF16)],
        [VMEM, VMEM],
        [pltpu.VMEM((2, CHUNK, 2 * NB), BF16), pltpu.SemaphoreType.DMA((2,))],
        flops=20 * NB * M,
        nbytes=4 * NB * M,
        out_specs=[HBM],
    )(obs_xy, xy)
    recv = exchange(piece, "z")
    (piece,) = call("pair", pair_kernel, [((XC, NZ // 2, S, CAP), F32)], [VMEM])(recv)
    recv = exchange(piece, ("x", "core"))
    return call("final", final_kernel, [((S, NB), F32)], [VMEM] * 3, flops=4 * 2 * S * NB * M, nbytes=4 * NB * M)(
        recv, tile, field
    )[0]


def solution(mesh):
    grid = Mesh(mesh.devices.reshape(NZ, 4, 2, 4), ("z", "x", "core", "y"))
    leaf = ("z", "x", "core")
    in_specs = (
        P("y", leaf),
        P(leaf, None),
        P(None, None, leaf),
        P(None, leaf),
        P(leaf),
        P(leaf),
        P(leaf),
        P(("z", "x", "core", "y"), None),
    )

    return jax.shard_map(body, mesh=grid, in_specs=in_specs, out_specs=P("y", leaf), check_vma=False)
```

time: 699 us -> 147 us (0.21)
  blocking collectives: 318 us -> 36.9 us
  waiting for transfers between devices: 237 us -> 22 us
  local copies, waits for them, and re-layouts: 91.2 us -> 15.3 us
  starting transfers between devices: 4.34 us -> 48.8 us
  matrix products: 28.1 us -> 0 us
  Pallas kernels: 0 us -> 21.8 us
  between operations: 14.2 us -> 0.86 us
    all_gather x2 -> x0, waiting for transfers between devices: 237 us -> none  [the longest x1 150 us: body(): everyone = lax.all_gather(project[None], 'leaf', axis=0, tiled=True)]
    all_gather x2 -> x0, blocking collectives: 217 us -> none  [the longest x1 110 us: body(): lax.all_gather(local_xy[None], ('leaf', 'obs'), axis=0, tiled=True)]
    unnamed x1 -> x0, blocking collectives: 102 us -> none
    gather x4 -> x0, local copies, waits for them, and re-layouts: 63.5 us -> none  [the longest x1 31.1 us: solve_rows(): resid_comp = resid_all[:, obs_index]]
    all_to_all x0 -> x2, blocking collectives: none -> 36.9 us  [exchange(): return lax.all_to_all(piece, axes, 0, 0, tiled=True)]
    all_to_all x1 -> x4, starting transfers between devices: 4.29 us -> 32.9 us  [exchange(): return lax.all_to_all(piece, axes, 0, 0, tiled=True)]
    pallas_call x0 -> x11, Pallas kernels: none -> 21.8 us  [the longest x1 10.4 us: body(): call('cross', cross_kernel, [((M, 2 * NB), BF16)], [VMEM, VMEM], [pltpu.V...]
    dot_general x12 -> x0, matrix products: 19.3 us -> none  [the longest x8 8.74 us: one_step(): jnp.dot(part_coef, tile, precision=lax.Precision.HIGHEST, preferred_eleme...]
  transfers between devices with their start and end apart: 3 -> 8, of which waited for: 2 -> 4; matrix products, arithmetic and copies ran while one was open for 6% -> 0% of each run, Pallas kernels for 0% -> 8%
where the time goes in v1:
time: 147 us; the launch traced here: 146 us
  starting transfers between devices  48.8 us (33%)
  blocking collectives  36.9 us (25%)
  waiting for transfers between devices  22 us (15%)
  Pallas kernels  21.8 us (15%)
  local copies, waits for them, and re-layouts  15.3 us (10%)
    all_to_all x2, blocking collectives, exchange(): return lax.all_to_all(piece, axes, 0, 0, tiled=True)  36.9 us
    all_to_all x4, starting transfers between devices, exchange(): return lax.all_to_all(piece, axes, 0, 0, tiled=True)  32.9 us
    unnamed x32, local copies, waits for them, and re-layouts  15.1 us
    all_to_all x4, waiting for transfers between devices, exchange(): return lax.all_to_all(piece, axes, 0, 0, tiled=True)  12.6 us
    pallas_call x1, Pallas kernels, body(): call('cross', cross_kernel, [((M, 2 * NB), BF16)], [VMEM, VMEM], [pltpu.V...  10.4 us
    ppermute x3, starting transfers between devices, body(): lax.ppermute(inverse_rows, 'y', [(y, y ^ d) for y in range(4)])  9.42 us
    ppermute x3, waiting for transfers between devices, body(): lax.ppermute(inverse_rows, 'y', [(y, y ^ d) for y in range(4)])  9.39 us
    ppermute x1, starting transfers between devices, body(): other = lax.ppermute(own, 'core', [(0, 1), (1, 0)])  6.47 us
  transfers between devices with their start and end apart: 8, of which 4 were waited for; matrix products, arithmetic and copies ran while one was open for 0% of the time, Pallas kernels for 8%

profile of v1, /device:TPU:1, one launch (start us, length us, event | category | flops | bytes accessed | tf_op | source)
XLA Modules:
  0.0 145.8 jit_solution(10015593687533016378)
XLA Ops:
  0.7 1.9 %shard_map.82 = f32[8,16,512]{2,1,0:T(8,128)} custom-call(bf16[16,256]{1,0:T(8,128)(2,1)} %z_ref.3, bf16[448,256]{1,0:T(8,128)(2,1)} %bitcast.3, s32[1]{0:T(128)S(6)} %copy.9.count_ref), custom_call_target="tpu_custom_call" | custom-call | tf_op jit(solution)/shard_map/pallas_call | solution.py:277
  2.5 10.2 %all-to-all-start = ((f32[8,16,512]{2,1,0:T(8,128)}), f32[8,16,512]{2,1,0:T(8,128)S(1)}, u32[]{:S(2)}, u32[]{:S(2)}) async-start(f32[8,16,512]{2,1,0:T(8,128)} %shard_map.82), calls=%async_computation | async-start | bytes 524288 | tf_op jit(solution)/shard_map/all_to_all | solution.py:268
  17.8 1.3 all-to-all-done.recv_ref
  19.9 10.5 %all-to-all-start.1 = ((f32[16,16,128]{2,1,0:T(8,128)}), f32[16,16,128]{2,1,0:T(8,128)S(1)}, u32[]{:S(2)}, u32[]{:S(2)}) async-start(f32[16,16,128]{2,1,0:T(8,128)} %get-tuple-element.17), calls=%async_computation.1 | async-start | bytes 262144 | tf_op jit(solution)/shard_map/all_to_all | solution.py:268
  31.1 11.3 %all-to-all-done.1.recv_ref.extra_ref = f32[16,16,128]{2,1,0:T(8,128)S(1)} async-done(((f32[16,16,128]{2,1,0:T(8,128)}), f32[16,16,128]{2,1,0:T(8,128)S(1)}, u32[]{:S(2)}, u32[]{:S(2)}) %all-to-all-start.1) | async-done | bytes 131104 | tf_op jit(solution)/shard_map/all_to_all | solution.py:268
  42.8 17.4 %all_to_all.30.recv_ref = f32[16,16,128]{2,1,0:T(8,128)S(1)} all-to-all(f32[16,16,128]{2,1,0:T(8,128)S(1)} %get-tuple-element.22), channel_id=1, replica_groups=mesh['z'=16,'x'=4,'core'=2,'y'=4] {'z'}, dimensions={0} | all-to-all | bytes 262144 | tf_op jit(solution)/shard_map/all_to_all | solution.py:268
  61.2 3.8 %all-to-all-start.3 = ((f32[4,288,128]{2,1,0:T(8,128)}), f32[4,288,128]{2,1,0:T(8,128)S(1)}, u32[]{:S(2)}, u32[]{:S(2)}) async-start(f32[4,288,128]{2,1,0:T(8,128)} %shard_map.87), calls=%async_computation.3 | async-start | bytes 1179648 | tf_op jit(solution)/shard_map/all_to_all | solution.py:268
  65.0 4.8 %collective-permute-start.2 = (f32[16,8192]{1,0:T(8,128)}, f32[16,8192]{1,0:T(8,128)S(1)}, u32[]{:S(2)}, u32[]{:S(2)}) collective-permute-start(f32[16,8192]{1,0:T(8,128)} %refs_0_.1), channel_id=1, source_target_pairs={{0,2},{1,3},{2,0},{3,1},{4,6},{5,7},{6,4},{7,5},{8,10},{9,11},{10,... | collective-permute-start | bytes 1572872 | tf_op jit(solution)/shard_map/ppermute | solution.py:275
  69.8 2.3 %collective-permute-start.1 = (f32[16,8192]{1,0:T(8,128)}, f32[16,8192]{1,0:T(8,128)S(1)}, u32[]{:S(2)}, u32[]{:S(2)}) collective-permute-start(f32[16,8192]{1,0:T(8,128)} %refs_0_.1), channel_id=1, source_target_pairs={{0,1},{1,0},{2,3},{3,2},{4,5},{5,4},{6,7},{7,6},{8,9},{9,8},{10,11... | collective-permute-start | bytes 1572872 | tf_op jit(solution)/shard_map/ppermute | solution.py:275
  72.2 2.3 %collective-permute-start.3 = (f32[16,8192]{1,0:T(8,128)}, f32[16,8192]{1,0:T(8,128)S(1)}, u32[]{:S(2)}, u32[]{:S(2)}) collective-permute-start(f32[16,8192]{1,0:T(8,128)} %refs_0_.1), channel_id=1, source_target_pairs={{0,3},{1,2},{2,1},{3,0},{4,7},{5,6},{6,5},{7,4},{8,11},{9,10},{10,... | collective-permute-start | bytes 1572872 | tf_op jit(solution)/shard_map/ppermute | solution.py:275
  74.5 6.5 %collective-permute-start = (f32[4,288,128]{2,1,0:T(8,128)S(1)}, f32[4,288,128]{2,1,0:T(8,128)S(1)}, u32[]{:S(2)}, u32[]{:S(2)}) collective-permute-start(f32[4,288,128]{2,1,0:T(8,128)S(1)} %all-to-all-done.3.own_ref), channel_id=1, source_target_pairs={{0,4},{4,0},{1,5},{5,1},{2,6},{6,2},{3,7},{7,3},{8,12},{12,8},{9,1... | collective-permute-start | bytes 1769480 | tf_op jit(solution)/shard_map/ppermute | solution.py:304
  81.8 7.9 %collective-permute-done.1.refs_1_ = f32[16,8192]{1,0:T(8,128)S(1)} collective-permute-done((f32[16,8192]{1,0:T(8,128)}, f32[16,8192]{1,0:T(8,128)S(1)}, u32[]{:S(2)}, u32[]{:S(2)}) %collective-permute-start.1) | collective-permute-done | bytes 524320 | tf_op jit(solution)/shard_map/ppermute | solution.py:275
  90.5 1.4 collective-permute-done.3.refs_3_
  92.8 1.0 copy-done.2
  93.8 1.0 copy-done.4
  94.9 1.0 copy-done.6
  95.9 1.0 copy-done.8
  96.9 1.3 shard_map.88.inv_ref
  98.6 2.4 %shard_map.89 = (f32[16,16,128]{2,1,0:T(8,128)S(1)}, f32[2,8448]{1,0:T(2,128)S(1)}) custom-call(s32[128]{0:T(128)S(1)} %convert_element_type.6.base_ref, s32[128]{0:T(128)S(1)} %convert_element_type.7.count_ref, f32[4,288,128]{2,1,0:T(8,128)S(1)} %all-to-all-done.3.own_ref, f32[4,288,128]{2,1,0:T(8,128)S(1)} %collective-permute-done.other_ref, ...), custom_call_target="tpu_custom_call" | custom-call | flops 67108864 | bytes 2097152 | tf_op jit(solution)/shard_map/pallas_call | solution.py:305
  101.0 19.5 %all_to_all.31.recv_ref = f32[16,16,128]{2,1,0:T(8,128)S(1)} all-to-all(f32[16,16,128]{2,1,0:T(8,128)S(1)} %get-tuple-element.23), channel_id=1, replica_groups=mesh['z'=16,'x'=4,'core'=2,'y'=4] {'z'}, dimensions={0} | all-to-all | bytes 262144 | tf_op jit(solution)/shard_map/all_to_all | solution.py:268
  121.5 8.4 %all-to-all-start.5 = ((f32[8,8,16,128]{3,2,1,0:T(8,128)}), f32[8,8,16,128]{3,2,1,0:T(8,128)S(1)}, u32[]{:S(2)}, u32[]{:S(2)}) async-start(f32[8,8,16,128]{3,2,1,0:T(8,128)} %shard_map.90), calls=%async_computation.5 | async-start | bytes 1048576 | tf_op jit(solution)/shard_map/all_to_all | solution.py:268
  129.9 10.4 %shard_map.91.tile_ref = bf16[8192,512]{1,0:T(8,128)(2,1)} custom-call(f32[2,8448]{1,0:T(2,128)} %copy-done.10, f32[2,256]{1,0:T(2,128)} %copy-done.13), custom_call_target="tpu_custom_call" | custom-call | flops 41943040 | bytes 8388608 | tf_op jit(solution)/shard_map/pallas_call | solution.py:314
  140.3 3.4 %copy-done = bf16[8192,512]{1,0:T(8,128)(2,1)S(1)} copy-done((bf16[8192,512]{1,0:T(8,128)(2,1)S(1)}, bf16[8192,512]{1,0:T(8,128)(2,1)}, u32[]{:S(2)}) %copy-start) | copy-done | bytes 8388632
  143.7 2.1 %shard_map.92 = f32[16,256]{1,0:T(8,128)} custom-call(f32[8,8,16,128]{3,2,1,0:T(8,128)S(1)} %all-to-all-done.5.recv_ref, bf16[8192,512]{1,0:T(8,128)(2,1)S(1)} %copy-done, f32[16,256]{1,0:T(8,128)S(1)} %get-tuple-element.26.field_ref), custom_call_target="tpu_custom_call" | custom-call | flops 268435456 | bytes 8388608 | tf_op jit(solution)/shard_map/pallas_call | solution.py:327
  (42 shorter events, 11.7 us)
Async XLA Ops:
  2.5 16.6 %all-to-all-start = ((f32[8,16,512]{2,1,0:T(8,128)}), f32[8,16,512]{2,1,0:T(8,128)S(1)}, u32[]{:S(2)}, u32[]{:S(2)}) async-start(f32[8,16,512]{2,1,0:T(8,128)} %shard_map.82), calls=%async_computation | async-start | bytes 524288 | tf_op jit(solution)/shard_map/all_to_all | solution.py:268
  12.7 0.9 copy-start.1
  13.6 0.9 copy-start.9
  14.5 0.7 copy-start.11
  15.2 0.7 copy-start.12
  15.9 0.7 copy-start.14
  17.2 0.6 copy-start.13
  19.9 22.5 %all-to-all-start.1 = ((f32[16,16,128]{2,1,0:T(8,128)}), f32[16,16,128]{2,1,0:T(8,128)S(1)}, u32[]{:S(2)}, u32[]{:S(2)}) async-start(f32[16,16,128]{2,1,0:T(8,128)} %get-tuple-element.17), calls=%async_computation.1 | async-start | bytes 262144 | tf_op jit(solution)/shard_map/all_to_all | solution.py:268
  30.5 0.7 copy-start.15
  61.2 13.2 %all-to-all-start.3 = ((f32[4,288,128]{2,1,0:T(8,128)}), f32[4,288,128]{2,1,0:T(8,128)S(1)}, u32[]{:S(2)}, u32[]{:S(2)}) async-start(f32[4,288,128]{2,1,0:T(8,128)} %shard_map.87), calls=%async_computation.3 | async-start | bytes 1179648 | tf_op jit(solution)/shard_map/all_to_all | solution.py:268
  65.0 15.9 %collective-permute-start.2 = (f32[16,8192]{1,0:T(8,128)}, f32[16,8192]{1,0:T(8,128)S(1)}, u32[]{:S(2)}, u32[]{:S(2)}) collective-permute-start(f32[16,8192]{1,0:T(8,128)} %refs_0_.1), channel_id=1, source_target_pairs={{0,2},{1,3},{2,0},{3,1},{4,6},{5,7},{6,4},{7,5},{8,10},{9,11},{10,... | collective-permute-start | bytes 1572872 | tf_op jit(solution)/shard_map/ppermute | solution.py:275
  69.8 19.9 %collective-permute-start.1 = (f32[16,8192]{1,0:T(8,128)}, f32[16,8192]{1,0:T(8,128)S(1)}, u32[]{:S(2)}, u32[]{:S(2)}) collective-permute-start(f32[16,8192]{1,0:T(8,128)} %refs_0_.1), channel_id=1, source_target_pairs={{0,1},{1,0},{2,3},{3,2},{4,5},{5,4},{6,7},{7,6},{8,9},{9,8},{10,11... | collective-permute-start | bytes 1572872 | tf_op jit(solution)/shard_map/ppermute | solution.py:275
  72.2 19.8 %collective-permute-start.3 = (f32[16,8192]{1,0:T(8,128)}, f32[16,8192]{1,0:T(8,128)S(1)}, u32[]{:S(2)}, u32[]{:S(2)}) collective-permute-start(f32[16,8192]{1,0:T(8,128)} %refs_0_.1), channel_id=1, source_target_pairs={{0,3},{1,2},{2,1},{3,0},{4,7},{5,6},{6,5},{7,4},{8,11},{9,10},{10,... | collective-permute-start | bytes 1572872 | tf_op jit(solution)/shard_map/ppermute | solution.py:275
  74.5 24.1 %collective-permute-start = (f32[4,288,128]{2,1,0:T(8,128)S(1)}, f32[4,288,128]{2,1,0:T(8,128)S(1)}, u32[]{:S(2)}, u32[]{:S(2)}) collective-permute-start(f32[4,288,128]{2,1,0:T(8,128)S(1)} %all-to-all-done.3.own_ref), channel_id=1, source_target_pairs={{0,4},{4,0},{1,5},{5,1},{2,6},{6,2},{3,7},{7,3},{8,12},{12,8},{9,1... | collective-permute-start | bytes 1769480 | tf_op jit(solution)/shard_map/ppermute | solution.py:304
  81.0 0.8 copy-start.3
  89.7 0.8 copy-start.5
  92.0 0.8 copy-start.7
  92.8 1.0 copy-start.2
  93.8 1.0 copy-start.4
  94.9 1.0 copy-start.6
  95.9 1.0 copy-start.8
  101.0 19.5 %copy-start.10 = (f32[2,8448]{1,0:T(2,128)}, f32[2,8448]{1,0:T(2,128)S(1)}, u32[]{:S(2)}) copy-start(f32[2,8448]{1,0:T(2,128)S(1)} %get-tuple-element.24.obs_ref) | copy-start | bytes 202756
  121.5 18.8 %all-to-all-start.5 = ((f32[8,8,16,128]{3,2,1,0:T(8,128)}), f32[8,8,16,128]{3,2,1,0:T(8,128)S(1)}, u32[]{:S(2)}, u32[]{:S(2)}) async-start(f32[8,8,16,128]{3,2,1,0:T(8,128)} %shard_map.90), calls=%async_computation.5 | async-start | bytes 1048576 | tf_op jit(solution)/shard_map/all_to_all | solution.py:268
  140.3 3.4 %copy-start = (bf16[8192,512]{1,0:T(8,128)(2,1)S(1)}, bf16[8192,512]{1,0:T(8,128)(2,1)}, u32[]{:S(2)}) copy-start(bf16[8192,512]{1,0:T(8,128)(2,1)} %shard_map.91.tile_ref) | copy-start | bytes 25165828

commit v2 on v1

--- a/solution.py
+++ b/solution.py
@@ -27,7 +27,7 @@
 SMEM = pl.BlockSpec(memory_space=pltpu.SMEM)
 NT = (((1,), (1,)), ((), ()))
 
-VMEM_MIB = {'local': 2, 'observed': 1, 'near': 2, 'field': 4, 'inverse': 8, 'spread': 4, 'coef': 10, 'cross': 60, 'pair': 4, 'final': 14}
+VMEM_MIB = {'local': 2, 'observed': 1, 'near': 2, 'field': 4, 'inverse': 10, 'join': 4, 'spread': 4, 'coef': 10, 'cross': 8, 'own_half': 14, 'other_half': 10}
 
 
 def dot(a, b, dims=(((1,), (0,)), ((), ()))):
@@ -139,13 +139,18 @@
             out_ref[x, S * NZ + 2 * z : S * NZ + 2 * z + 8] = rows
 
 
-def inverse_kernel(*refs):
-    *blocks, out_ref = refs
+def join_kernel(own_hbm, next_hbm, out_hbm, held, sems):
+    fetch(sems, [(own_hbm, held.at[0]), (next_hbm, held.at[1])])
+    fetch(sems, [(held.at[d], out_hbm.at[d]) for d in range(2)])
+
+
+def inverse_kernel(near_hbm, far_hbm, out_ref, held, sems):
+    fetch(sems, [(ref.at[d], held.at[2 * i + d]) for i, ref in enumerate((near_hbm, far_hbm)) for d in range(2)])
     my_y = lax.axis_index("y")
 
     def one_part(j, carry):
         at = pl.multiple_of(j * 256, 256)
-        got = [ref[:, pl.ds(at, 256)] for ref in blocks]
+        got = [held[d, :, pl.ds(at, 256)] for d in range(4)]
         rows = []
         for y in range(4):
             apart = my_y ^ y
@@ -186,38 +191,42 @@
     for k in range(0, M, width):
         acc = acc + dot(jnp.concatenate(split2(packed[:, k : k + width]), axis=0), inv_ref[k : k + width])
     coef = acc[:S] + acc[S:]
-    piece = jnp.concatenate([coef[:, :ROWS] + coef[:, ROWS:], jnp.zeros((S, CAP - ROWS), F32)], axis=1)
-    for z in range(NZ):
-        out_ref[z] = piece
-
-
-def pair_kernel(recv_ref, out_ref):
-    for k in range(NZ // 2):
-        pair = jnp.concatenate([recv_ref[2 * k][:, :ROWS], recv_ref[2 * k + 1][:, :ROWS]], axis=1)
-        for q in range(XC):
-            out_ref[q, k] = pair
-
-
-CHUNK = 512
-
-
-def cross_kernel(obs_ref, xy_ref, out_hbm, buf, sems):
+    coef = coef[:, :ROWS] + coef[:, ROWS:]
+    piece = jnp.concatenate([coef[: S // 2], coef[S // 2 :]], axis=1)
+    for i in range(M // CAP):
+        out_ref[i] = piece
+
+
+HALF = M // 2
+CHUNK = 256
+KEPT = 10
+
+
+def cross_kernel(obs_ref, xy_ref, kept_ref, own_hbm, other_hbm, buf, sems):
+    core = lax.axis_index("core")
     sx = xy_ref[0:1] * SCALE
     sy = xy_ref[1:2] * SCALE
 
-    def copy(i, slot):
-        return pltpu.make_async_copy(buf.at[slot], out_hbm.at[pl.ds(pl.multiple_of(i * CHUNK, CHUNK), CHUNK)], sems.at[slot])
-
-    def two_chunks(j, carry):
-        for slot in range(2):
-            i = 2 * j + slot
-
-            @pl.when(j > 0)
+    def rows(i):
+        return pl.ds(pl.multiple_of(i * CHUNK, CHUNK), CHUNK)
+
+    def copies(i, slot, own_ref, first):
+        return [
+            pltpu.make_async_copy(buf.at[slot, 0], own_ref.at[rows(i - first)], sems.at[slot, 0]),
+            pltpu.make_async_copy(buf.at[slot, 1], other_hbm.at[rows(i)], sems.at[slot, 1]),
+        ]
+
+    def step(own_ref, first):
+        def run(i, carry):
+            slot = i % 2
+
+            @pl.when(i > 1)
             def _():
-                copy(i - 2, slot).wait()
-
-            for row in range(0, CHUNK, CAP):
-                at = pl.multiple_of(i * CHUNK + row, CAP)
+                for copy in copies(first, slot, own_ref, first):
+                    copy.wait()
+
+            for m in range(4):
+                at = pl.multiple_of(2 * CHUNK * i + CAP * m, CAP)
                 ox = jnp.transpose(jnp.broadcast_to(obs_ref[0:1, pl.ds(at, CAP)], (CAP, CAP)))
                 oy = jnp.transpose(jnp.broadcast_to(obs_ref[1:2, pl.ds(at, CAP)], (CAP, CAP)))
                 for h in range(0, NB, CAP):
@@ -225,44 +234,85 @@
                     dy = oy - sy[:, h : h + CAP]
                     square = jnp.maximum(dx * dx + dy * dy, 1e-30)
                     hi, lo = split2(jnp.exp2(-(square * lax.rsqrt(square))))
-                    buf[slot, row : row + CAP, h : h + CAP] = hi
-                    buf[slot, row : row + CAP, NB + h : NB + h + CAP] = lo
-            copy(i, slot).start()
-        return carry
-
-    steps = M // CHUNK
-    lax.fori_loop(0, steps // 2, two_chunks, 0)
-    for slot in range(2):
-        copy(steps - 2 + slot, slot).wait()
-
-
-def final_kernel(recv_ref, tile_ref, field_ref, out_ref):
-    lane = lax.broadcasted_iota(jnp.int32, (S, CAP), 1)
+                    for c in range(2):
+                        for part, left in ((hi, h), (lo, NB + h)):
+                            buf[slot, core ^ c, ROWS * m : ROWS * (m + 1), left : left + CAP] = part[ROWS * c : ROWS * (c + 1)]
+            for copy in copies(i, slot, own_ref, first):
+                copy.start()
+            return carry
+
+        return run
+
+    steps = HALF // CHUNK
+    lax.fori_loop(0, KEPT, step(kept_ref, 0), 0)
+    lax.fori_loop(KEPT, steps, step(own_hbm, KEPT), 0)
+    for i in range(steps - 2, steps):
+        for copy in copies(i, i % 2, own_hbm, KEPT):
+            copy.wait()
+
+
+def coef_chunk(pieces_ref, k):
+    lane = lax.broadcasted_iota(jnp.int32, (S // 2, CAP), 1)
+    blocks = []
+    for m in range(4 * k, 4 * k + 4, 2):
+        even, odd = pieces_ref[m], pieces_ref[m + 1]
+        first = jnp.where(lane < ROWS, even, pltpu.roll(odd, ROWS, 1))
+        second = jnp.where(lane < ROWS, pltpu.roll(even, ROWS, 1), odd)
+        blocks.append(jnp.concatenate([first, second], axis=0))
+    return jnp.concatenate(split2(jnp.concatenate(blocks, axis=1)), axis=0)
+
+
+def fold(acc):
+    acc = acc[:S] + acc[S:]
+    return acc[:, :NB] + acc[:, NB:]
+
+
+def own_half_kernel(pieces_ref, kept_ref, own_hbm, other_hbm, out_ref, other_ref, buf, sems, other_sem):
+    steps = HALF // CHUNK
+    rows = [pl.ds(i * CHUNK, CHUNK) for i in range(steps)]
+    copies = [pltpu.make_async_copy(own_hbm.at[rows[i]], buf.at[i], sems.at[i]) for i in range(steps - KEPT)]
+    others = [pltpu.make_async_copy(other_hbm.at[rows[i]], other_ref.at[rows[i]], other_sem.at[i]) for i in range(steps)]
+    for copy in copies + others:
+        copy.start()
     acc = jnp.zeros((2 * S, 2 * NB), F32)
-    for k in range(NZ // 2):
-        first, second = [], []
-        for x in range(XC // 2):
-            even, odd = recv_ref[2 * x, k], recv_ref[2 * x + 1, k]
-            first.append(jnp.where(lane < ROWS, even, pltpu.roll(odd, ROWS, 1)))
-            second.append(jnp.where(lane < ROWS, pltpu.roll(even, ROWS, 1), odd))
-        left = jnp.concatenate(split2(jnp.concatenate(first + second, axis=1)), axis=0)
-        acc = acc + dot(left, tile_ref[1024 * k : 1024 * (k + 1)])
-    acc = acc[:S] + acc[S:]
-    out_ref[...] = field_ref[...] + (acc[:, :NB] + acc[:, NB:])
+    for k in range(steps):
+        left = coef_chunk(pieces_ref, k)
+        if k < KEPT:
+            right = kept_ref[rows[k]]
+        else:
+            copies[k - KEPT].wait()
+            right = buf[k - KEPT]
+        acc = acc + dot(left, right)
+    out_ref[...] = fold(acc)
+    for copy in others:
+        copy.wait()
+
+
+def other_half_kernel(pieces_ref, tile_ref, partial_ref, field_ref, out_ref):
+    acc = jnp.zeros((2 * S, 2 * NB), F32)
+    for k in range(HALF // CHUNK):
+        acc = acc + dot(coef_chunk(pieces_ref, k), tile_ref[k * CHUNK : (k + 1) * CHUNK])
+    out_ref[...] = field_ref[...] + (partial_ref[...] + fold(acc))
 
 
 def call(name, kernel, out, specs, scratch=(), flops=0, nbytes=0, out_specs=None):
-    shapes = [jax.ShapeDtypeStruct(s, d) for s, d in out]
-    return pl.pallas_call(
+    out_specs = out_specs or [VMEM] * len(out)
+    shapes = [pltpu.MemorySpace.HBM(s, d) if spec is HBM else jax.ShapeDtypeStruct(s, d) for (s, d), spec in zip(out, out_specs)]
+    made = pl.pallas_call(
         kernel,
         out_shape=shapes,
         in_specs=specs,
-        out_specs=out_specs or [VMEM] * len(shapes),
+        out_specs=out_specs,
         scratch_shapes=list(scratch),
         compiler_params=pltpu.CompilerParams(vmem_limit_bytes=VMEM_MIB[name] << 20 if name in VMEM_MIB else None),
         cost_estimate=pl.CostEstimate(flops=flops, bytes_accessed=nbytes, transcendentals=0),
     )
 
+    def run(*args):
+        return made(*(pltpu.with_memory_space_constraint(a, pltpu.MemorySpace.HBM) if spec is HBM else a for a, spec in zip(args, specs)))
+
+    return run
+
 
 def exchange(piece, axes):
     return lax.all_to_all(piece, axes, 0, 0, tiled=True)
@@ -270,9 +320,16 @@
 
 def body(samples_z, diag_block, level_basis, site_xy, obs_site, obs_value, obs_count, inverse_rows):
     basis = level_basis.reshape(LEVELS * R, NB)
-    blocks = [inverse_rows]
-    for d in (1, 2, 3):
-        blocks.append(lax.ppermute(inverse_rows, "y", [(y, y ^ d) for y in range(4)]))
+    block = lax.ppermute(inverse_rows, "y", [(y, y ^ 1) for y in range(4)])
+    (pair,) = call(
+        "join",
+        join_kernel,
+        [((2, S, M), F32)],
+        [HBM, HBM],
+        [pltpu.VMEM((2, S, M), F32), pltpu.SemaphoreType.DMA((2,))],
+        out_specs=[HBM],
+    )(inverse_rows, block)
+    far_pair = lax.ppermute(pair, "y", [(y, y ^ 2) for y in range(4)])
 
     (piece,) = call("project", project_kernel, [((XC, S, 512), F32)], [VMEM, VMEM, SMEM])(samples_z, basis, obs_count)
     recv = exchange(piece, ("x", "core"))
@@ -296,8 +353,14 @@
         extra, near, local, basis, pick, value
     )
     (inv,) = call(
-        "inverse", inverse_kernel, [((M, 2 * ROWS), BF16)], [VMEM] * 4, flops=20 * ROWS * M, nbytes=8 * ROWS * M
-    )(*blocks)
+        "inverse",
+        inverse_kernel,
+        [((M, 2 * ROWS), BF16)],
+        [HBM] * 2,
+        [pltpu.VMEM((4, S, M), F32), pltpu.SemaphoreType.DMA((4,))],
+        flops=20 * ROWS * M,
+        nbytes=8 * ROWS * M,
+    )(pair, far_pair)
     recv = exchange(piece, "z")
     (piece,) = call("spread", spread_kernel, [((4, 18 * NZ, CAP), F32)], [VMEM] * 2)(recv, extra)
     own = exchange(piece, "x")
@@ -305,27 +368,40 @@
     piece, obs_xy = call(
         "coef",
         coef_kernel,
-        [((NZ, S, CAP), F32), ((2, M + 2 * CAP), F32)],
+        [((M // CAP, S // 2, CAP), F32), ((2, M + 2 * CAP), F32)],
         [SMEM, SMEM, VMEM, VMEM, VMEM],
         [pltpu.VMEM((S, M + 2 * CAP), F32)],
         flops=4 * 2 * S * ROWS * M,
         nbytes=4 * ROWS * M,
     )(base, counts, own, other, inv)
-    (tile,) = call(
+    kept, own_tile, other_tile = call(
         "cross",
         cross_kernel,
-        [((M, 2 * NB), BF16)],
+        [((KEPT * CHUNK, 2 * NB), BF16), ((HALF - KEPT * CHUNK, 2 * NB), BF16), ((HALF, 2 * NB), BF16)],
         [VMEM, VMEM],
-        [pltpu.VMEM((2, CHUNK, 2 * NB), BF16), pltpu.SemaphoreType.DMA((2,))],
+        [pltpu.VMEM((2, 2, CHUNK, 2 * NB), BF16), pltpu.SemaphoreType.DMA((2, 2))],
         flops=20 * NB * M,
         nbytes=4 * NB * M,
-        out_specs=[HBM],
+        out_specs=[VMEM, HBM, HBM],
     )(obs_xy, xy)
-    recv = exchange(piece, "z")
-    (piece,) = call("pair", pair_kernel, [((XC, NZ // 2, S, CAP), F32)], [VMEM])(recv)
-    recv = exchange(piece, ("x", "core"))
-    return call("final", final_kernel, [((S, NB), F32)], [VMEM] * 3, flops=4 * 2 * S * NB * M, nbytes=4 * NB * M)(
-        recv, tile, field
+    own = exchange(piece, ("z", "x"))
+    other = lax.ppermute(own, "core", [(0, 1), (1, 0)])
+    streamed = HALF // CHUNK - KEPT
+    partial, other_tile = call(
+        "own_half",
+        own_half_kernel,
+        [((S, NB), F32), ((HALF, 2 * NB), BF16)],
+        [VMEM, VMEM, HBM, HBM],
+        [
+            pltpu.VMEM((streamed, CHUNK, 2 * NB), BF16),
+            pltpu.SemaphoreType.DMA((streamed,)),
+            pltpu.SemaphoreType.DMA((HALF // CHUNK,)),
+        ],
+        flops=2 * 2 * S * NB * M,
+        nbytes=4 * NB * M,
+    )(own, kept, own_tile, other_tile)
+    return call("other_half", other_half_kernel, [((S, NB), F32)], [VMEM] * 4, flops=2 * 2 * S * NB * M, nbytes=2 * NB * M)(
+        other, other_tile, partial, field
     )[0]
 
 

time: 147 us -> 138 us (0.939)
  local copies, waits for them, and re-layouts: 15.3 us -> 2.77 us
  waiting for transfers between devices: 22 us -> 17 us
  Pallas kernels: 21.8 us -> 26.7 us
  blocking collectives: 36.9 us -> 40.8 us
    unnamed x32 -> x6, local copies, waits for them, and re-layouts: 15.1 us -> 2.52 us
    ppermute x3 -> x2, waiting for transfers between devices: 9.39 us -> 0.33 us  [the longest x1 0.32 us: body(): far_pair = lax.ppermute(pair, 'y', [(y, y ^ 2) for y in range(4)])]
    ppermute x1 -> x2, starting transfers between devices: 6.47 us -> 14.7 us  [body(): other = lax.ppermute(own, 'core', [(0, 1), (1, 0)])]
    all_to_all x4 -> x3, starting transfers between devices: 32.9 us -> 26.4 us  [exchange(): return lax.all_to_all(piece, axes, 0, 0, tiled=True)]
    pallas_call x11 -> x12, Pallas kernels: 21.8 us -> 26.7 us  [run(): made(*(pltpu.with_memory_space_constraint(a, pltpu.MemorySpace.HBM) if sp...]
    all_to_all x4 -> x3, waiting for transfers between devices: 12.6 us -> 16.7 us  [exchange(): return lax.all_to_all(piece, axes, 0, 0, tiled=True)]
    all_to_all x2, blocking collectives: 36.9 us -> 40.8 us  [exchange(): return lax.all_to_all(piece, axes, 0, 0, tiled=True)]
    ppermute x3 -> x2, starting transfers between devices: 9.42 us -> 8.03 us  [the longest x1 4.82 us: body(): far_pair = lax.ppermute(pair, 'y', [(y, y ^ 2) for y in range(4)])]
  transfers between devices with their start and end apart: 8 -> 7, of which waited for: 4 -> 4; matrix products, arithmetic and copies ran while one was open for 0% -> 0% of each run, Pallas kernels for 8% -> 15%
where the time goes in v2:
time: 138 us; the launch traced here: 137 us
  starting transfers between devices  49.1 us (36%)
  blocking collectives  40.8 us (30%)
  Pallas kernels  26.7 us (19%)
  waiting for transfers between devices  17 us (12%)
  local copies, waits for them, and re-layouts  2.77 us (2%)
    all_to_all x2, blocking collectives, exchange(): return lax.all_to_all(piece, axes, 0, 0, tiled=True)  40.8 us
    pallas_call x12, Pallas kernels, run(): made(*(pltpu.with_memory_space_constraint(a, pltpu.MemorySpace.HBM) if sp...  26.7 us
    all_to_all x3, starting transfers between devices, exchange(): return lax.all_to_all(piece, axes, 0, 0, tiled=True)  26.4 us
    all_to_all x3, waiting for transfers between devices, exchange(): return lax.all_to_all(piece, axes, 0, 0, tiled=True)  16.7 us
    ppermute x2, starting transfers between devices, body(): other = lax.ppermute(own, 'core', [(0, 1), (1, 0)])  14.7 us
    ppermute x1, starting transfers between devices, body(): far_pair = lax.ppermute(pair, 'y', [(y, y ^ 2) for y in range(4)])  4.82 us
    ppermute x1, starting transfers between devices, body(): block = lax.ppermute(inverse_rows, 'y', [(y, y ^ 1) for y in range(4)])  3.21 us
  transfers between devices with their start and end apart: 7, of which 4 were waited for; matrix products, arithmetic and copies ran while one was open for 0% of the time, Pallas kernels for 15%

profile of v2, /device:TPU:1, one launch (start us, length us, event | category | flops | bytes accessed | tf_op | source)
XLA Modules:
  0.0 137.3 jit_solution(1478296022325234002)
XLA Ops:
  0.7 1.8 %shard_map.82 = f32[8,16,512]{2,1,0:T(8,128)} custom-call(bf16[16,256]{1,0:T(8,128)(2,1)} %z_ref.3, bf16[448,256]{1,0:T(8,128)(2,1)} %bitcast.3, s32[1]{0:T(128)S(6)} %copy.9.count_ref), custom_call_target="tpu_custom_call" | custom-call | tf_op jit(solution)/shard_map/pallas_call | solution.py:312
  2.5 10.2 %all-to-all-start = ((f32[8,16,512]{2,1,0:T(8,128)}), f32[8,16,512]{2,1,0:T(8,128)S(1)}, u32[]{:S(2)}, u32[]{:S(2)}) async-start(f32[8,16,512]{2,1,0:T(8,128)} %shard_map.82), calls=%async_computation | async-start | bytes 524288 | tf_op jit(solution)/shard_map/all_to_all | solution.py:318
  13.3 1.3 shard_map.83
  14.6 4.5 %all-to-all-done.recv_ref = f32[8,16,512]{2,1,0:T(8,128)S(1)} async-done(((f32[8,16,512]{2,1,0:T(8,128)}), f32[8,16,512]{2,1,0:T(8,128)S(1)}, u32[]{:S(2)}, u32[]{:S(2)}) %all-to-all-start) | async-done | bytes 262176 | tf_op jit(solution)/shard_map/all_to_all | solution.py:318
  19.1 0.8 shard_map.84
  19.9 10.5 %all-to-all-start.1 = ((f32[16,16,128]{2,1,0:T(8,128)}), f32[16,16,128]{2,1,0:T(8,128)S(1)}, u32[]{:S(2)}, u32[]{:S(2)}) async-start(f32[16,16,128]{2,1,0:T(8,128)} %get-tuple-element.22), calls=%async_computation.1 | async-start | bytes 262144 | tf_op jit(solution)/shard_map/all_to_all | solution.py:318
  30.5 3.2 %collective-permute-start.1 = (f32[16,8192]{1,0:T(8,128)}, f32[16,8192]{1,0:T(8,128)S(1)}, u32[]{:S(2)}, u32[]{:S(2)}) collective-permute-start(f32[16,8192]{1,0:T(8,128)} %own_hbm.1), channel_id=1, source_target_pairs={{0,1},{1,0},{2,3},{3,2},{4,5},{5,4},{6,7},{7,6},{8,9},{9,8},{10,11... | collective-permute-start | bytes 1572872 | tf_op jit(solution)/shard_map/ppermute | solution.py:323
  34.3 8.1 %all-to-all-done.1.recv_ref.extra_ref = f32[16,16,128]{2,1,0:T(8,128)S(1)} async-done(((f32[16,16,128]{2,1,0:T(8,128)}), f32[16,16,128]{2,1,0:T(8,128)S(1)}, u32[]{:S(2)}, u32[]{:S(2)}) %all-to-all-start.1) | async-done | bytes 131104 | tf_op jit(solution)/shard_map/all_to_all | solution.py:318
  42.4 1.0 shard_map.86
  43.5 5.7 %all-to-all-start.2 = ((f32[16,16,128]{2,1,0:T(8,128)}), f32[16,16,128]{2,1,0:T(8,128)S(1)}, u32[]{:S(2)}, u32[]{:S(2)}) async-start(f32[16,16,128]{2,1,0:T(8,128)} %get-tuple-element.27), calls=%async_computation.2 | async-start | bytes 262144 | tf_op jit(solution)/shard_map/all_to_all | solution.py:318
  49.2 0.8 copy-done.2
  50.0 2.2 %shard_map.88.near_hbm = f32[2,16,8192]{2,1,0:T(8,128)} custom-call(f32[16,8192]{1,0:T(8,128)} %own_hbm.1, f32[16,8192]{1,0:T(8,128)} %copy-done.2), custom_call_target="tpu_custom_call" | custom-call | tf_op jit(solution)/shard_map/pallas_call | solution.py:312
  52.2 4.8 %collective-permute-start.2 = (f32[2,16,8192]{2,1,0:T(8,128)}, f32[2,16,8192]{2,1,0:T(8,128)S(1)}, u32[]{:S(2)}, u32[]{:S(2)}) collective-permute-start(f32[2,16,8192]{2,1,0:T(8,128)} %shard_map.88.near_hbm), channel_id=1, source_target_pairs={{0,2},{1,3},{2,0},{3,1},{4,6},{5,7},{6,4},{7,5},{8,10},{9,11},{10,... | collective-permute-start | bytes 3145736 | tf_op jit(solution)/shard_map/ppermute | solution.py:332
  57.0 4.1 %all-to-all-done.2.recv_ref = f32[16,16,128]{2,1,0:T(8,128)S(1)} async-done(((f32[16,16,128]{2,1,0:T(8,128)}), f32[16,16,128]{2,1,0:T(8,128)S(1)}, u32[]{:S(2)}, u32[]{:S(2)}) %all-to-all-start.2) | async-done | bytes 131104 | tf_op jit(solution)/shard_map/all_to_all | solution.py:318
  61.2 10.0 %all_to_all.25.own_ref = f32[4,288,128]{2,1,0:T(8,128)S(1)} all-to-all(f32[4,288,128]{2,1,0:T(8,128)S(1)} %shard_map.87), channel_id=1, replica_groups=mesh['z'=16,'x'=4,'core'=2,'y'=4] {'x'}, dimensions={0} | all-to-all | bytes 1179648 | tf_op jit(solution)/shard_map/all_to_all | solution.py:318
  71.2 6.7 %collective-permute-start = (f32[4,288,128]{2,1,0:T(8,128)S(1)}, f32[4,288,128]{2,1,0:T(8,128)S(1)}, u32[]{:S(2)}, u32[]{:S(2)}) collective-permute-start(f32[4,288,128]{2,1,0:T(8,128)S(1)} %all_to_all.25.own_ref), channel_id=1, source_target_pairs={{0,4},{4,0},{1,5},{5,1},{2,6},{6,2},{3,7},{7,3},{8,12},{12,8},{9,1... | collective-permute-start | bytes 1769480 | tf_op jit(solution)/shard_map/ppermute | solution.py:367
  78.7 1.0 copy-done.1
  79.7 2.8 %shard_map.89.inv_ref = bf16[8192,128]{1,0:T(8,128)(2,1)S(1)} custom-call(f32[2,16,8192]{2,1,0:T(8,128)} %shard_map.88.near_hbm, f32[2,16,8192]{2,1,0:T(8,128)} %copy-done.1), custom_call_target="tpu_custom_call" | custom-call | flops 10485760 | bytes 4194304 | tf_op jit(solution)/shard_map/pallas_call | solution.py:312
  82.5 2.5 %shard_map.90 = (f32[64,8,128]{2,1,0:T(8,128)S(1)}, f32[2,8448]{1,0:T(2,128)S(1)}) custom-call(s32[128]{0:T(128)S(1)} %convert_element_type.6.base_ref, s32[128]{0:T(128)S(1)} %convert_element_type.7.count_ref, f32[4,288,128]{2,1,0:T(8,128)S(1)} %all_to_all.25.own_ref, f32[4,288,128]{2,1,0:T(8,128)S(1)} %collective-permute-done.other_ref, ...), custom_call_target="tpu_custom_call" | custom-call | flops 67108864 | bytes 2097152 | tf_op jit(solution)/shard_map/pallas_call | solution.py:312
  85.0 30.8 %all_to_all.26.pieces_ref = f32[64,8,128]{2,1,0:T(8,128)S(1)} all-to-all(f32[64,8,128]{2,1,0:T(8,128)S(1)} %get-tuple-element.28), channel_id=1, replica_groups=mesh['z'=16,'x'=4,'core'=2,'y'=4] {'z','x'}, dimensions={0} | all-to-all | bytes 524288 | tf_op jit(solution)/shard_map/all_to_all | solution.py:318
  115.8 8.0 %collective-permute-start.3 = (f32[64,8,128]{2,1,0:T(8,128)S(1)}, f32[64,8,128]{2,1,0:T(8,128)S(1)}, u32[]{:S(2)}, u32[]{:S(2)}) collective-permute-start(f32[64,8,128]{2,1,0:T(8,128)S(1)} %all_to_all.26.pieces_ref), channel_id=1, source_target_pairs={{0,4},{4,0},{1,5},{5,1},{2,6},{6,2},{3,7},{7,3},{8,12},{12,8},{9,1... | collective-permute-start | bytes 786440 | tf_op jit(solution)/shard_map/ppermute | solution.py:388
  123.8 9.2 %shard_map.91 = (bf16[2560,512]{1,0:T(8,128)(2,1)S(1)}, bf16[1536,512]{1,0:T(8,128)(2,1)}, bf16[4096,512]{1,0:T(8,128)(2,1)}) custom-call(f32[2,8448]{1,0:T(2,128)S(1)} %get-tuple-element.29.obs_ref, f32[2,256]{1,0:T(2,128)S(1)} %get-tuple-element.30.xy_ref), custom_call_target="tpu_custom_call" | custom-call | flops 41943040 | bytes 8388608 | tf_op jit(solution)/shard_map/pallas_call | solution.py:312
  132.9 2.9 %shard_map.92 = (f32[16,256]{1,0:T(8,128)S(1)}, bf16[4096,512]{1,0:T(8,128)(2,1)S(1)}) custom-call(f32[64,8,128]{2,1,0:T(8,128)S(1)} %all_to_all.26.pieces_ref, bf16[2560,512]{1,0:T(8,128)(2,1)S(1)} %get-tuple-element.31.kept_ref, bf16[1536,512]{1,0:T(8,128)(2,1)} %get-tuple-element.32.own_hbm, bf16[4096,512]{1,0:T(8,128)(2,1)} %get-tuple-element.33.other_hbm), custom_call_target="tpu_custom_call" | custom-call | flops 134217728 | bytes 8388608 | tf_op jit(solution)/shard_map/pallas_call | solution.py:312
  135.9 1.4 %shard_map.93 = f32[16,256]{1,0:T(8,128)} custom-call(f32[64,8,128]{2,1,0:T(8,128)S(1)} %collective-permute-done.3.pieces_ref, bf16[4096,512]{1,0:T(8,128)(2,1)S(1)} %get-tuple-element.34.tile_ref, f32[16,256]{1,0:T(8,128)S(1)} %get-tuple-element.35.partial_ref, f32[16,256]{1,0:T(8,128)S(1)} %get-tuple-element.36.field_ref), custom_call_target="tpu_custom_call" | custom-call | flops 134217728 | bytes 4194304 | tf_op jit(solution)/shard_map/pallas_call | solution.py:312
  (15 shorter events, 2.2 us)
Async XLA Ops:
  2.5 16.6 %all-to-all-start = ((f32[8,16,512]{2,1,0:T(8,128)}), f32[8,16,512]{2,1,0:T(8,128)S(1)}, u32[]{:S(2)}, u32[]{:S(2)}) async-start(f32[8,16,512]{2,1,0:T(8,128)} %shard_map.82), calls=%async_computation | async-start | bytes 524288 | tf_op jit(solution)/shard_map/all_to_all | solution.py:318
  12.6 0.7 copy-start
  19.9 22.5 %all-to-all-start.1 = ((f32[16,16,128]{2,1,0:T(8,128)}), f32[16,16,128]{2,1,0:T(8,128)S(1)}, u32[]{:S(2)}, u32[]{:S(2)}) async-start(f32[16,16,128]{2,1,0:T(8,128)} %get-tuple-element.22), calls=%async_computation.1 | async-start | bytes 262144 | tf_op jit(solution)/shard_map/all_to_all | solution.py:318
  30.5 18.7 %collective-permute-start.1 = (f32[16,8192]{1,0:T(8,128)}, f32[16,8192]{1,0:T(8,128)S(1)}, u32[]{:S(2)}, u32[]{:S(2)}) collective-permute-start(f32[16,8192]{1,0:T(8,128)} %own_hbm.1), channel_id=1, source_target_pairs={{0,1},{1,0},{2,3},{3,2},{4,5},{5,4},{6,7},{7,6},{8,9},{9,8},{10,11... | collective-permute-start | bytes 1572872 | tf_op jit(solution)/shard_map/ppermute | solution.py:323
  43.5 17.7 %all-to-all-start.2 = ((f32[16,16,128]{2,1,0:T(8,128)}), f32[16,16,128]{2,1,0:T(8,128)S(1)}, u32[]{:S(2)}, u32[]{:S(2)}) async-start(f32[16,16,128]{2,1,0:T(8,128)} %get-tuple-element.27), calls=%async_computation.2 | async-start | bytes 262144 | tf_op jit(solution)/shard_map/all_to_all | solution.py:318
  49.2 0.8 copy-start.2
  52.2 26.5 %collective-permute-start.2 = (f32[2,16,8192]{2,1,0:T(8,128)}, f32[2,16,8192]{2,1,0:T(8,128)S(1)}, u32[]{:S(2)}, u32[]{:S(2)}) collective-permute-start(f32[2,16,8192]{2,1,0:T(8,128)} %shard_map.88.near_hbm), channel_id=1, source_target_pairs={{0,2},{1,3},{2,0},{3,1},{4,6},{5,7},{6,4},{7,5},{8,10},{9,11},{10,... | collective-permute-start | bytes 3145736 | tf_op jit(solution)/shard_map/ppermute | solution.py:332
  71.2 11.3 %collective-permute-start = (f32[4,288,128]{2,1,0:T(8,128)S(1)}, f32[4,288,128]{2,1,0:T(8,128)S(1)}, u32[]{:S(2)}, u32[]{:S(2)}) collective-permute-start(f32[4,288,128]{2,1,0:T(8,128)S(1)} %all_to_all.25.own_ref), channel_id=1, source_target_pairs={{0,4},{4,0},{1,5},{5,1},{2,6},{6,2},{3,7},{7,3},{8,12},{12,8},{9,1... | collective-permute-start | bytes 1769480 | tf_op jit(solution)/shard_map/ppermute | solution.py:367
  78.6 1.0 copy-start.1
  115.8 20.1 %collective-permute-start.3 = (f32[64,8,128]{2,1,0:T(8,128)S(1)}, f32[64,8,128]{2,1,0:T(8,128)S(1)}, u32[]{:S(2)}, u32[]{:S(2)}) collective-permute-start(f32[64,8,128]{2,1,0:T(8,128)S(1)} %all_to_all.26.pieces_ref), channel_id=1, source_target_pairs={{0,4},{4,0},{1,5},{5,1},{2,6},{6,2},{3,7},{7,3},{8,12},{12,8},{9,1... | collective-permute-start | bytes 786440 | tf_op jit(solution)/shard_map/ppermute | solution.py:388

commit v3 on v2

--- a/solution.py
+++ b/solution.py
@@ -27,7 +27,7 @@
 SMEM = pl.BlockSpec(memory_space=pltpu.SMEM)
 NT = (((1,), (1,)), ((), ()))
 
-VMEM_MIB = {'local': 2, 'observed': 1, 'near': 2, 'field': 4, 'inverse': 10, 'join': 4, 'spread': 4, 'coef': 10, 'cross': 8, 'own_half': 14, 'other_half': 10}
+VMEM_MIB = {'local': 2, 'near': 2, 'field': 4, 'inverse': 10, 'join': 4, 'spread': 4, 'coef': 10, 'cross': 8, 'own_half': 14, 'other_half': 10}
 
 
 def dot(a, b, dims=(((1,), (0,)), ((), ()))):
@@ -62,14 +62,10 @@
         out_ref[q] = piece
 
 
-def observed_kernel(value_hbm, value_ref, sems):
-    fetch(sems, [(value_hbm, value_ref)])
-
-
 def local_kernel(
-    z_ref, diag_hbm, xy_hbm, site_hbm, basis_hbm, field_ref, pick_ref, xy_at_ref, xy_ref, basis_ref, diag_ref, site_ref, sems
+    z_ref, diag_hbm, xy_hbm, site_hbm, basis_hbm, value_hbm, field_ref, pick_ref, xy_at_ref, xy_ref, basis_ref, value_ref, diag_ref, site_ref, sems
 ):
-    fetch(sems, [(diag_hbm, diag_ref), (xy_hbm, xy_ref), (site_hbm, site_ref), (basis_hbm, basis_ref)])
+    fetch(sems, [(diag_hbm, diag_ref), (xy_hbm, xy_ref), (site_hbm, site_ref), (basis_hbm, basis_ref), (value_hbm, value_ref)])
     field_ref[...] = dot(z_ref[...], diag_ref[...])
     site = lax.broadcasted_iota(jnp.int32, (NB, CAP), 0)
     pick = jnp.where(site == site_ref[...], 1.0, 0.0).astype(BF16)
@@ -139,9 +135,12 @@
             out_ref[x, S * NZ + 2 * z : S * NZ + 2 * z + 8] = rows
 
 
-def join_kernel(own_hbm, next_hbm, out_hbm, held, sems):
-    fetch(sems, [(own_hbm, held.at[0]), (next_hbm, held.at[1])])
-    fetch(sems, [(held.at[d], out_hbm.at[d]) for d in range(2)])
+def join_kernel(own_hbm, next_ref, out_hbm, held, sems):
+    arrived = pltpu.make_async_copy(next_ref, out_hbm.at[1], sems.at[1])
+    arrived.start()
+    fetch(sems, [(own_hbm, held)])
+    fetch(sems, [(held, out_hbm.at[0])])
+    arrived.wait()
 
 
 def inverse_kernel(near_hbm, far_hbm, out_ref, held, sems):
@@ -199,7 +198,7 @@
 
 HALF = M // 2
 CHUNK = 256
-KEPT = 10
+KEPT = 12
 
 
 def cross_kernel(obs_ref, xy_ref, kept_ref, own_hbm, other_hbm, buf, sems):
@@ -325,24 +324,23 @@
         "join",
         join_kernel,
         [((2, S, M), F32)],
-        [HBM, HBM],
-        [pltpu.VMEM((2, S, M), F32), pltpu.SemaphoreType.DMA((2,))],
+        [HBM, VMEM],
+        [pltpu.VMEM((S, M), F32), pltpu.SemaphoreType.DMA((2,))],
         out_specs=[HBM],
     )(inverse_rows, block)
     far_pair = lax.ppermute(pair, "y", [(y, y ^ 2) for y in range(4)])
 
     (piece,) = call("project", project_kernel, [((XC, S, 512), F32)], [VMEM, VMEM, SMEM])(samples_z, basis, obs_count)
     recv = exchange(piece, ("x", "core"))
-    local, pick, xy_at, xy, basis = call(
+    local, pick, xy_at, xy, basis, value = call(
         "local",
         local_kernel,
-        [((S, NB), F32), ((NB, CAP), BF16), ((S, R), F32), ((2, NB), F32), ((LEVELS * R, NB), BF16)],
-        [VMEM] + [HBM] * 4,
-        [pltpu.VMEM((NB, NB), BF16), pltpu.VMEM((1, CAP), jnp.int32), pltpu.SemaphoreType.DMA((4,))],
+        [((S, NB), F32), ((NB, CAP), BF16), ((S, R), F32), ((2, NB), F32), ((LEVELS * R, NB), BF16), ((1, CAP), F32)],
+        [VMEM] + [HBM] * 5,
+        [pltpu.VMEM((NB, NB), BF16), pltpu.VMEM((1, CAP), jnp.int32), pltpu.SemaphoreType.DMA((5,))],
         flops=2 * S * NB * NB,
         nbytes=1 << 18,
-    )(samples_z, diag_block, site_xy, obs_site.reshape(1, CAP), basis)
-    (value,) = call("observed", observed_kernel, [((1, CAP), F32)], [HBM], [pltpu.SemaphoreType.DMA((1,))])(obs_value.reshape(1, CAP))
+    )(samples_z, diag_block, site_xy, obs_site.reshape(1, CAP), basis, obs_value.reshape(1, CAP))
     near, piece = call("near", near_kernel, [((S, 512), F32), ((NZ, S, CAP), F32)], [VMEM] * 2)(recv, xy_at)
     extra = exchange(piece, "z")
     counts = extra[:, 8:, R].reshape(XC * NZ)

time: 138 us -> 137 us (level)
    all_to_all x3, waiting for transfers between devices: 16.7 us -> 18.3 us  [exchange(): return lax.all_to_all(piece, axes, 0, 0, tiled=True)]
    pallas_call x12 -> x11, Pallas kernels: 26.7 us -> 25.7 us  [run(): made(*(pltpu.with_memory_space_constraint(a, pltpu.MemorySpace.HBM) if sp...]
  transfers between devices with their start and end apart: 7 -> 7, of which waited for: 4 -> 3; matrix products, arithmetic and copies ran while one was open for 0% -> 0% of each run, Pallas kernels for 15% -> 14%
where the time goes in v3:
time: 137 us; the launch traced here: 136 us
  starting transfers between devices  49.1 us (36%)
  blocking collectives  40.1 us (29%)
  Pallas kernels  25.7 us (19%)
  waiting for transfers between devices  18.3 us (13%)
  local copies, waits for them, and re-layouts  1.94 us (1%)
    all_to_all x2, blocking collectives, exchange(): return lax.all_to_all(piece, axes, 0, 0, tiled=True)  40.1 us
    all_to_all x3, starting transfers between devices, exchange(): return lax.all_to_all(piece, axes, 0, 0, tiled=True)  26.4 us
    pallas_call x11, Pallas kernels, run(): made(*(pltpu.with_memory_space_constraint(a, pltpu.MemorySpace.HBM) if sp...  25.7 us
    all_to_all x3, waiting for transfers between devices, exchange(): return lax.all_to_all(piece, axes, 0, 0, tiled=True)  18.3 us
    ppermute x2, starting transfers between devices, body(): other = lax.ppermute(own, 'core', [(0, 1), (1, 0)])  14.7 us
    ppermute x1, starting transfers between devices, body(): far_pair = lax.ppermute(pair, 'y', [(y, y ^ 2) for y in range(4)])  4.82 us
    ppermute x1, starting transfers between devices, body(): block = lax.ppermute(inverse_rows, 'y', [(y, y ^ 1) for y in range(4)])  3.21 us
  transfers between devices with their start and end apart: 7, of which 3 were waited for; matrix products, arithmetic and copies ran while one was open for 0% of the time, Pallas kernels for 14%

profile of v3, /device:TPU:1, one launch (start us, length us, event | category | flops | bytes accessed | tf_op | source)
XLA Modules:
  0.0 136.2 jit_solution(9118238165641289485)
XLA Ops:
  0.7 1.9 %shard_map.82 = f32[8,16,512]{2,1,0:T(8,128)} custom-call(bf16[16,256]{1,0:T(8,128)(2,1)} %z_ref.3, bf16[448,256]{1,0:T(8,128)(2,1)} %bitcast.3, s32[1]{0:T(128)S(6)} %copy.9.count_ref), custom_call_target="tpu_custom_call" | custom-call | tf_op jit(solution)/shard_map/pallas_call | solution.py:311
  2.5 10.2 %all-to-all-start = ((f32[8,16,512]{2,1,0:T(8,128)}), f32[8,16,512]{2,1,0:T(8,128)S(1)}, u32[]{:S(2)}, u32[]{:S(2)}) async-start(f32[8,16,512]{2,1,0:T(8,128)} %shard_map.82), calls=%async_computation | async-start | bytes 524288 | tf_op jit(solution)/shard_map/all_to_all | solution.py:317
  12.7 0.7 copy-done
  13.4 1.3 shard_map.83
  14.7 4.5 %all-to-all-done.recv_ref = f32[8,16,512]{2,1,0:T(8,128)S(1)} async-done(((f32[8,16,512]{2,1,0:T(8,128)}), f32[8,16,512]{2,1,0:T(8,128)S(1)}, u32[]{:S(2)}, u32[]{:S(2)}) %all-to-all-start) | async-done | bytes 262176 | tf_op jit(solution)/shard_map/all_to_all | solution.py:317
  19.2 0.8 shard_map.84
  19.9 10.5 %all-to-all-start.1 = ((f32[16,16,128]{2,1,0:T(8,128)}), f32[16,16,128]{2,1,0:T(8,128)S(1)}, u32[]{:S(2)}, u32[]{:S(2)}) async-start(f32[16,16,128]{2,1,0:T(8,128)} %get-tuple-element.23), calls=%async_computation.1 | async-start | bytes 262144 | tf_op jit(solution)/shard_map/all_to_all | solution.py:317
  30.5 3.2 %collective-permute-start.1 = (f32[16,8192]{1,0:T(8,128)}, f32[16,8192]{1,0:T(8,128)S(1)}, u32[]{:S(2)}, u32[]{:S(2)}) collective-permute-start(f32[16,8192]{1,0:T(8,128)} %own_hbm.1), channel_id=1, source_target_pairs={{0,1},{1,0},{2,3},{3,2},{4,5},{5,4},{6,7},{7,6},{8,9},{9,8},{10,11... | collective-permute-start | bytes 1572872 | tf_op jit(solution)/shard_map/ppermute | solution.py:322
  33.7 8.7 %all-to-all-done.1.recv_ref.extra_ref = f32[16,16,128]{2,1,0:T(8,128)S(1)} async-done(((f32[16,16,128]{2,1,0:T(8,128)}), f32[16,16,128]{2,1,0:T(8,128)S(1)}, u32[]{:S(2)}, u32[]{:S(2)}) %all-to-all-start.1) | async-done | bytes 131104 | tf_op jit(solution)/shard_map/all_to_all | solution.py:317
  42.4 1.0 shard_map.85
  43.5 5.7 %all-to-all-start.2 = ((f32[16,16,128]{2,1,0:T(8,128)}), f32[16,16,128]{2,1,0:T(8,128)S(1)}, u32[]{:S(2)}, u32[]{:S(2)}) async-start(f32[16,16,128]{2,1,0:T(8,128)} %get-tuple-element.29), calls=%async_computation.2 | async-start | bytes 262144 | tf_op jit(solution)/shard_map/all_to_all | solution.py:317
  49.2 2.1 %shard_map.87.near_hbm = f32[2,16,8192]{2,1,0:T(8,128)} custom-call(f32[16,8192]{1,0:T(8,128)} %own_hbm.1, f32[16,8192]{1,0:T(8,128)S(1)} %collective-permute-done.1.next_ref), custom_call_target="tpu_custom_call" | custom-call | tf_op jit(solution)/shard_map/pallas_call | solution.py:311
  51.2 4.8 %collective-permute-start.2 = (f32[2,16,8192]{2,1,0:T(8,128)}, f32[2,16,8192]{2,1,0:T(8,128)S(1)}, u32[]{:S(2)}, u32[]{:S(2)}) collective-permute-start(f32[2,16,8192]{2,1,0:T(8,128)} %shard_map.87.near_hbm), channel_id=1, source_target_pairs={{0,2},{1,3},{2,0},{3,1},{4,6},{5,7},{6,4},{7,5},{8,10},{9,11},{10,... | collective-permute-start | bytes 3145736 | tf_op jit(solution)/shard_map/ppermute | solution.py:331
  56.1 5.1 %all-to-all-done.2.recv_ref = f32[16,16,128]{2,1,0:T(8,128)S(1)} async-done(((f32[16,16,128]{2,1,0:T(8,128)}), f32[16,16,128]{2,1,0:T(8,128)S(1)}, u32[]{:S(2)}, u32[]{:S(2)}) %all-to-all-start.2) | async-done | bytes 131104 | tf_op jit(solution)/shard_map/all_to_all | solution.py:317
  61.2 10.0 %all_to_all.25.own_ref = f32[4,288,128]{2,1,0:T(8,128)S(1)} all-to-all(f32[4,288,128]{2,1,0:T(8,128)S(1)} %shard_map.86), channel_id=1, replica_groups=mesh['z'=16,'x'=4,'core'=2,'y'=4] {'x'}, dimensions={0} | all-to-all | bytes 1179648 | tf_op jit(solution)/shard_map/all_to_all | solution.py:317
  71.2 6.7 %collective-permute-start = (f32[4,288,128]{2,1,0:T(8,128)S(1)}, f32[4,288,128]{2,1,0:T(8,128)S(1)}, u32[]{:S(2)}, u32[]{:S(2)}) collective-permute-start(f32[4,288,128]{2,1,0:T(8,128)S(1)} %all_to_all.25.own_ref), channel_id=1, source_target_pairs={{0,4},{4,0},{1,5},{5,1},{2,6},{6,2},{3,7},{7,3},{8,12},{12,8},{9,1... | collective-permute-start | bytes 1769480 | tf_op jit(solution)/shard_map/ppermute | solution.py:365
  78.4 1.0 copy-done.1
  79.4 2.8 %shard_map.88.inv_ref = bf16[8192,128]{1,0:T(8,128)(2,1)S(1)} custom-call(f32[2,16,8192]{2,1,0:T(8,128)} %shard_map.87.near_hbm, f32[2,16,8192]{2,1,0:T(8,128)} %copy-done.1), custom_call_target="tpu_custom_call" | custom-call | flops 10485760 | bytes 4194304 | tf_op jit(solution)/shard_map/pallas_call | solution.py:311
  82.2 2.5 %shard_map.89 = (f32[64,8,128]{2,1,0:T(8,128)S(1)}, f32[2,8448]{1,0:T(2,128)S(1)}) custom-call(s32[128]{0:T(128)S(1)} %convert_element_type.6.base_ref, s32[128]{0:T(128)S(1)} %convert_element_type.7.count_ref, f32[4,288,128]{2,1,0:T(8,128)S(1)} %all_to_all.25.own_ref, f32[4,288,128]{2,1,0:T(8,128)S(1)} %collective-permute-done.other_ref, ...), custom_call_target="tpu_custom_call" | custom-call | flops 67108864 | bytes 2097152 | tf_op jit(solution)/shard_map/pallas_call | solution.py:311
  84.7 30.2 %all_to_all.26.pieces_ref = f32[64,8,128]{2,1,0:T(8,128)S(1)} all-to-all(f32[64,8,128]{2,1,0:T(8,128)S(1)} %get-tuple-element.30), channel_id=1, replica_groups=mesh['z'=16,'x'=4,'core'=2,'y'=4] {'z','x'}, dimensions={0} | all-to-all | bytes 524288 | tf_op jit(solution)/shard_map/all_to_all | solution.py:317
  114.8 8.0 %collective-permute-start.3 = (f32[64,8,128]{2,1,0:T(8,128)S(1)}, f32[64,8,128]{2,1,0:T(8,128)S(1)}, u32[]{:S(2)}, u32[]{:S(2)}) collective-permute-start(f32[64,8,128]{2,1,0:T(8,128)S(1)} %all_to_all.26.pieces_ref), channel_id=1, source_target_pairs={{0,4},{4,0},{1,5},{5,1},{2,6},{6,2},{3,7},{7,3},{8,12},{12,8},{9,1... | collective-permute-start | bytes 786440 | tf_op jit(solution)/shard_map/ppermute | solution.py:386
  122.8 9.1 %shard_map.90 = (bf16[3072,512]{1,0:T(8,128)(2,1)S(1)}, bf16[1024,512]{1,0:T(8,128)(2,1)}, bf16[4096,512]{1,0:T(8,128)(2,1)}) custom-call(f32[2,8448]{1,0:T(2,128)S(1)} %get-tuple-element.31.obs_ref, f32[2,256]{1,0:T(2,128)S(1)} %get-tuple-element.32.xy_ref), custom_call_target="tpu_custom_call" | custom-call | flops 41943040 | bytes 8388608 | tf_op jit(solution)/shard_map/pallas_call | solution.py:311
  131.9 2.8 %shard_map.91 = (f32[16,256]{1,0:T(8,128)S(1)}, bf16[4096,512]{1,0:T(8,128)(2,1)S(1)}) custom-call(f32[64,8,128]{2,1,0:T(8,128)S(1)} %all_to_all.26.pieces_ref, bf16[3072,512]{1,0:T(8,128)(2,1)S(1)} %get-tuple-element.33.kept_ref, bf16[1024,512]{1,0:T(8,128)(2,1)} %get-tuple-element.34.own_hbm, bf16[4096,512]{1,0:T(8,128)(2,1)} %get-tuple-element.35.other_hbm), custom_call_target="tpu_custom_call" | custom-call | flops 134217728 | bytes 8388608 | tf_op jit(solution)/shard_map/pallas_call | solution.py:311
  134.7 1.4 %shard_map.92 = f32[16,256]{1,0:T(8,128)} custom-call(f32[64,8,128]{2,1,0:T(8,128)S(1)} %collective-permute-done.3.pieces_ref, bf16[4096,512]{1,0:T(8,128)(2,1)S(1)} %get-tuple-element.36.tile_ref, f32[16,256]{1,0:T(8,128)S(1)} %get-tuple-element.37.partial_ref, f32[16,256]{1,0:T(8,128)S(1)} %get-tuple-element.38.field_ref), custom_call_target="tpu_custom_call" | custom-call | flops 134217728 | bytes 4194304 | tf_op jit(solution)/shard_map/pallas_call | solution.py:311
  (12 shorter events, 0.5 us)
Async XLA Ops:
  2.5 16.6 %all-to-all-start = ((f32[8,16,512]{2,1,0:T(8,128)}), f32[8,16,512]{2,1,0:T(8,128)S(1)}, u32[]{:S(2)}, u32[]{:S(2)}) async-start(f32[8,16,512]{2,1,0:T(8,128)} %shard_map.82), calls=%async_computation | async-start | bytes 524288 | tf_op jit(solution)/shard_map/all_to_all | solution.py:317
  12.7 0.7 copy-start
  19.9 22.5 %all-to-all-start.1 = ((f32[16,16,128]{2,1,0:T(8,128)}), f32[16,16,128]{2,1,0:T(8,128)S(1)}, u32[]{:S(2)}, u32[]{:S(2)}) async-start(f32[16,16,128]{2,1,0:T(8,128)} %get-tuple-element.23), calls=%async_computation.1 | async-start | bytes 262144 | tf_op jit(solution)/shard_map/all_to_all | solution.py:317
  30.5 18.7 %collective-permute-start.1 = (f32[16,8192]{1,0:T(8,128)}, f32[16,8192]{1,0:T(8,128)S(1)}, u32[]{:S(2)}, u32[]{:S(2)}) collective-permute-start(f32[16,8192]{1,0:T(8,128)} %own_hbm.1), channel_id=1, source_target_pairs={{0,1},{1,0},{2,3},{3,2},{4,5},{5,4},{6,7},{7,6},{8,9},{9,8},{10,11... | collective-permute-start | bytes 1572872 | tf_op jit(solution)/shard_map/ppermute | solution.py:322
  43.5 17.7 %all-to-all-start.2 = ((f32[16,16,128]{2,1,0:T(8,128)}), f32[16,16,128]{2,1,0:T(8,128)S(1)}, u32[]{:S(2)}, u32[]{:S(2)}) async-start(f32[16,16,128]{2,1,0:T(8,128)} %get-tuple-element.29), calls=%async_computation.2 | async-start | bytes 262144 | tf_op jit(solution)/shard_map/all_to_all | solution.py:317
  51.2 27.1 %collective-permute-start.2 = (f32[2,16,8192]{2,1,0:T(8,128)}, f32[2,16,8192]{2,1,0:T(8,128)S(1)}, u32[]{:S(2)}, u32[]{:S(2)}) collective-permute-start(f32[2,16,8192]{2,1,0:T(8,128)} %shard_map.87.near_hbm), channel_id=1, source_target_pairs={{0,2},{1,3},{2,0},{3,1},{4,6},{5,7},{6,4},{7,5},{8,10},{9,11},{10,... | collective-permute-start | bytes 3145736 | tf_op jit(solution)/shard_map/ppermute | solution.py:331
  71.2 11.0 %collective-permute-start = (f32[4,288,128]{2,1,0:T(8,128)S(1)}, f32[4,288,128]{2,1,0:T(8,128)S(1)}, u32[]{:S(2)}, u32[]{:S(2)}) collective-permute-start(f32[4,288,128]{2,1,0:T(8,128)S(1)} %all_to_all.25.own_ref), channel_id=1, source_target_pairs={{0,4},{4,0},{1,5},{5,1},{2,6},{6,2},{3,7},{7,3},{8,12},{12,8},{9,1... | collective-permute-start | bytes 1769480 | tf_op jit(solution)/shard_map/ppermute | solution.py:365
  78.3 1.0 copy-start.1
  114.8 19.9 %collective-permute-start.3 = (f32[64,8,128]{2,1,0:T(8,128)S(1)}, f32[64,8,128]{2,1,0:T(8,128)S(1)}, u32[]{:S(2)}, u32[]{:S(2)}) collective-permute-start(f32[64,8,128]{2,1,0:T(8,128)S(1)} %all_to_all.26.pieces_ref), channel_id=1, source_target_pairs={{0,4},{4,0},{1,5},{5,1},{2,6},{6,2},{3,7},{7,3},{8,12},{12,8},{9,1... | collective-permute-start | bytes 786440 | tf_op jit(solution)/shard_map/ppermute | solution.py:386

commit v4 on v3

--- a/solution.py
+++ b/solution.py
@@ -27,7 +27,7 @@
 SMEM = pl.BlockSpec(memory_space=pltpu.SMEM)
 NT = (((1,), (1,)), ((), ()))
 
-VMEM_MIB = {'local': 2, 'near': 2, 'field': 4, 'inverse': 10, 'join': 4, 'spread': 4, 'coef': 10, 'cross': 8, 'own_half': 14, 'other_half': 10}
+VMEM_MIB = {'local': 2, 'near': 2, 'field': 4, 'inverse': 10, 'join': 4, 'spread': 4, 'pack': 4, 'coef': 10, 'cross': 8, 'own_half': 14, 'other_half': 10}
 
 
 def dot(a, b, dims=(((1,), (0,)), ((), ()))):
@@ -63,9 +63,9 @@
 
 
 def local_kernel(
-    z_ref, diag_hbm, xy_hbm, site_hbm, basis_hbm, value_hbm, field_ref, pick_ref, xy_at_ref, xy_ref, basis_ref, value_ref, diag_ref, site_ref, sems
+    z_hbm, diag_hbm, xy_hbm, site_hbm, basis_hbm, value_hbm, field_ref, pick_ref, xy_at_ref, xy_ref, basis_ref, value_ref, diag_ref, site_ref, z_ref, sems
 ):
-    fetch(sems, [(diag_hbm, diag_ref), (xy_hbm, xy_ref), (site_hbm, site_ref), (basis_hbm, basis_ref), (value_hbm, value_ref)])
+    fetch(sems, [(diag_hbm, diag_ref), (xy_hbm, xy_ref), (site_hbm, site_ref), (basis_hbm, basis_ref), (value_hbm, value_ref), (z_hbm, z_ref)])
     field_ref[...] = dot(z_ref[...], diag_ref[...])
     site = lax.broadcasted_iota(jnp.int32, (NB, CAP), 0)
     pick = jnp.where(site == site_ref[...], 1.0, 0.0).astype(BF16)
@@ -162,29 +162,35 @@
     lax.fori_loop(0, M // 256, one_part, 0, unroll=4)
 
 
-def coef_kernel(base_ref, count_ref, own_ref, other_ref, inv_ref, out_ref, xy_ref, packed):
-    core = lax.axis_index("core")
+def pack(base_ref, count_ref, ref, c, packed, xy_ref):
     lane = lax.broadcasted_iota(jnp.int32, (S, CAP), 1)
 
     def one_column(x, carry):
-        for ref, c in ((own_ref, core), (other_ref, 1 - core)):
-            for z in range(NZ):
-                p = 8 * z + 2 * x + c
-                base, count = base_ref[p], count_ref[p]
-                shift = base % CAP
-                start = pl.multiple_of(base - shift, CAP)
-                end = shift + count
-                first = (lane >= shift) & (lane < end)
-                second = lane < end - CAP
-                got = pltpu.roll(ref[x, S * z : S * (z + 1)], shift, 1)
-                pltpu.store(packed.at[:, pl.ds(start, CAP)], got, mask=first)
-                pltpu.store(packed.at[:, pl.ds(start + CAP, CAP)], got, mask=second)
-                got = pltpu.roll(ref[x, S * NZ + 2 * z : S * NZ + 2 * z + 2], shift, 1)
-                pltpu.store(xy_ref.at[:, pl.ds(start, CAP)], got, mask=first[:2])
-                pltpu.store(xy_ref.at[:, pl.ds(start + CAP, CAP)], got, mask=second[:2])
+        for z in range(NZ):
+            p = 8 * z + 2 * x + c
+            base, count = base_ref[p], count_ref[p]
+            shift = base % CAP
+            start = pl.multiple_of(base - shift, CAP)
+            end = shift + count
+            first = (lane >= shift) & (lane < end)
+            second = lane < end - CAP
+            got = pltpu.roll(ref[x, S * z : S * (z + 1)], shift, 1)
+            pltpu.store(packed.at[:, pl.ds(start, CAP)], got, mask=first)
+            pltpu.store(packed.at[:, pl.ds(start + CAP, CAP)], got, mask=second)
+            got = pltpu.roll(ref[x, S * NZ + 2 * z : S * NZ + 2 * z + 2], shift, 1)
+            pltpu.store(xy_ref.at[:, pl.ds(start, CAP)], got, mask=first[:2])
+            pltpu.store(xy_ref.at[:, pl.ds(start + CAP, CAP)], got, mask=second[:2])
         return carry
 
     lax.fori_loop(0, 4, one_column, 0)
+
+
+def pack_kernel(base_ref, count_ref, own_ref, packed, xy_ref):
+    pack(base_ref, count_ref, own_ref, lax.axis_index("core"), packed, xy_ref)
+
+
+def coef_kernel(base_ref, count_ref, other_ref, inv_ref, packed_in, xy_in, packed, xy_ref, out_ref):
+    pack(base_ref, count_ref, other_ref, 1 - lax.axis_index("core"), packed, xy_ref)
     acc = jnp.zeros((2 * S, 2 * ROWS), F32)
     width = 1024
     for k in range(0, M, width):
@@ -294,7 +300,7 @@
     out_ref[...] = field_ref[...] + (partial_ref[...] + fold(acc))
 
 
-def call(name, kernel, out, specs, scratch=(), flops=0, nbytes=0, out_specs=None):
+def call(name, kernel, out, specs, scratch=(), flops=0, nbytes=0, out_specs=None, aliases=None):
     out_specs = out_specs or [VMEM] * len(out)
     shapes = [pltpu.MemorySpace.HBM(s, d) if spec is HBM else jax.ShapeDtypeStruct(s, d) for (s, d), spec in zip(out, out_specs)]
     made = pl.pallas_call(
@@ -303,6 +309,7 @@
         in_specs=specs,
         out_specs=out_specs,
         scratch_shapes=list(scratch),
+        input_output_aliases=aliases or {},
         compiler_params=pltpu.CompilerParams(vmem_limit_bytes=VMEM_MIB[name] << 20 if name in VMEM_MIB else None),
         cost_estimate=pl.CostEstimate(flops=flops, bytes_accessed=nbytes, transcendentals=0),
     )
@@ -336,8 +343,8 @@
         "local",
         local_kernel,
         [((S, NB), F32), ((NB, CAP), BF16), ((S, R), F32), ((2, NB), F32), ((LEVELS * R, NB), BF16), ((1, CAP), F32)],
-        [VMEM] + [HBM] * 5,
-        [pltpu.VMEM((NB, NB), BF16), pltpu.VMEM((1, CAP), jnp.int32), pltpu.SemaphoreType.DMA((5,))],
+        [HBM] * 6,
+        [pltpu.VMEM((NB, NB), BF16), pltpu.VMEM((1, CAP), jnp.int32), pltpu.VMEM((S, NB), BF16), pltpu.SemaphoreType.DMA((6,))],
         flops=2 * S * NB * NB,
         nbytes=1 << 18,
     )(samples_z, diag_block, site_xy, obs_site.reshape(1, CAP), basis, obs_value.reshape(1, CAP))
@@ -363,15 +370,17 @@
     (piece,) = call("spread", spread_kernel, [((4, 18 * NZ, CAP), F32)], [VMEM] * 2)(recv, extra)
     own = exchange(piece, "x")
     other = lax.ppermute(own, "core", [(0, 1), (1, 0)])
-    piece, obs_xy = call(
+    width = M + 2 * CAP
+    packed, obs_xy = call("pack", pack_kernel, [((S, width), F32), ((2, width), F32)], [SMEM, SMEM, VMEM])(base, counts, own)
+    _, obs_xy, piece = call(
         "coef",
         coef_kernel,
-        [((M // CAP, S // 2, CAP), F32), ((2, M + 2 * CAP), F32)],
-        [SMEM, SMEM, VMEM, VMEM, VMEM],
-        [pltpu.VMEM((S, M + 2 * CAP), F32)],
+        [((S, width), F32), ((2, width), F32), ((M // CAP, S // 2, CAP), F32)],
+        [SMEM, SMEM] + [VMEM] * 4,
         flops=4 * 2 * S * ROWS * M,
         nbytes=4 * ROWS * M,
-    )(base, counts, own, other, inv)
+        aliases={4: 0, 5: 1},
+    )(base, counts, other, inv, packed, obs_xy)
     kept, own_tile, other_tile = call(
         "cross",
         cross_kernel,

time: 137 us -> 137 us (level)
    pallas_call x11 -> x12, Pallas kernels: 25.7 us -> 26.3 us  [run(): made(*(pltpu.with_memory_space_constraint(a, pltpu.MemorySpace.HBM) if sp...]
  transfers between devices with their start and end apart: 7 -> 7, of which waited for: 3 -> 3; matrix products, arithmetic and copies ran while one was open for 0% -> 0% of each run, Pallas kernels for 14% -> 15%
where the time goes in v4:
time: 137 us
  starting transfers between devices  49.1 us (36%)
  blocking collectives  40.1 us (29%)
  Pallas kernels  26.3 us (19%)
  waiting for transfers between devices  19 us (14%)
    all_to_all x2, blocking collectives, exchange(): return lax.all_to_all(piece, axes, 0, 0, tiled=True)  40.1 us
    all_to_all x3, starting transfers between devices, exchange(): return lax.all_to_all(piece, axes, 0, 0, tiled=True)  26.4 us
    pallas_call x12, Pallas kernels, run(): made(*(pltpu.with_memory_space_constraint(a, pltpu.MemorySpace.HBM) if sp...  26.3 us
    all_to_all x3, waiting for transfers between devices, exchange(): return lax.all_to_all(piece, axes, 0, 0, tiled=True)  19 us
    ppermute x2, starting transfers between devices, body(): other = lax.ppermute(own, 'core', [(0, 1), (1, 0)])  14.7 us
    ppermute x1, starting transfers between devices, body(): far_pair = lax.ppermute(pair, 'y', [(y, y ^ 2) for y in range(4)])  4.82 us
    ppermute x1, starting transfers between devices, body(): block = lax.ppermute(inverse_rows, 'y', [(y, y ^ 1) for y in range(4)])  3.21 us
  transfers between devices with their start and end apart: 7, of which 3 were waited for; matrix products, arithmetic and copies ran while one was open for 0% of the time, Pallas kernels for 15%

profile of v4, /device:TPU:1, one launch (start us, length us, event | category | flops | bytes accessed | tf_op | source)
XLA Modules:
  0.0 136.7 jit_solution(16906736547492178532)
XLA Ops:
  0.7 1.9 %shard_map.82 = f32[8,16,512]{2,1,0:T(8,128)} custom-call(bf16[16,256]{1,0:T(8,128)(2,1)} %z_hbm.1, bf16[448,256]{1,0:T(8,128)(2,1)} %bitcast.3, s32[1]{0:T(128)S(6)} %copy.13.count_ref), custom_call_target="tpu_custom_call" | custom-call | tf_op jit(solution)/shard_map/pallas_call | solution.py:318
  2.5 10.2 %all-to-all-start = ((f32[8,16,512]{2,1,0:T(8,128)}), f32[8,16,512]{2,1,0:T(8,128)S(1)}, u32[]{:S(2)}, u32[]{:S(2)}) async-start(f32[8,16,512]{2,1,0:T(8,128)} %shard_map.82), calls=%async_computation | async-start | bytes 524288 | tf_op jit(solution)/shard_map/all_to_all | solution.py:324
  12.7 1.3 shard_map.83
  14.0 5.2 %all-to-all-done.recv_ref = f32[8,16,512]{2,1,0:T(8,128)S(1)} async-done(((f32[8,16,512]{2,1,0:T(8,128)}), f32[8,16,512]{2,1,0:T(8,128)S(1)}, u32[]{:S(2)}, u32[]{:S(2)}) %all-to-all-start) | async-done | bytes 262176 | tf_op jit(solution)/shard_map/all_to_all | solution.py:324
  19.2 0.8 shard_map.84
  19.9 10.5 %all-to-all-start.1 = ((f32[16,16,128]{2,1,0:T(8,128)}), f32[16,16,128]{2,1,0:T(8,128)S(1)}, u32[]{:S(2)}, u32[]{:S(2)}) async-start(f32[16,16,128]{2,1,0:T(8,128)} %get-tuple-element.25), calls=%async_computation.1 | async-start | bytes 262144 | tf_op jit(solution)/shard_map/all_to_all | solution.py:324
  30.5 3.2 %collective-permute-start.1 = (f32[16,8192]{1,0:T(8,128)}, f32[16,8192]{1,0:T(8,128)S(1)}, u32[]{:S(2)}, u32[]{:S(2)}) collective-permute-start(f32[16,8192]{1,0:T(8,128)} %own_hbm.1), channel_id=1, source_target_pairs={{0,1},{1,0},{2,3},{3,2},{4,5},{5,4},{6,7},{7,6},{8,9},{9,8},{10,11... | collective-permute-start | bytes 1572872 | tf_op jit(solution)/shard_map/ppermute | solution.py:329
  33.7 8.7 %all-to-all-done.1.recv_ref.extra_ref = f32[16,16,128]{2,1,0:T(8,128)S(1)} async-done(((f32[16,16,128]{2,1,0:T(8,128)}), f32[16,16,128]{2,1,0:T(8,128)S(1)}, u32[]{:S(2)}, u32[]{:S(2)}) %all-to-all-start.1) | async-done | bytes 131104 | tf_op jit(solution)/shard_map/all_to_all | solution.py:324
  42.4 1.0 shard_map.85
  43.5 5.7 %all-to-all-start.2 = ((f32[16,16,128]{2,1,0:T(8,128)}), f32[16,16,128]{2,1,0:T(8,128)S(1)}, u32[]{:S(2)}, u32[]{:S(2)}) async-start(f32[16,16,128]{2,1,0:T(8,128)} %get-tuple-element.31), calls=%async_computation.2 | async-start | bytes 262144 | tf_op jit(solution)/shard_map/all_to_all | solution.py:324
  49.2 2.1 %shard_map.87.near_hbm = f32[2,16,8192]{2,1,0:T(8,128)} custom-call(f32[16,8192]{1,0:T(8,128)} %own_hbm.1, f32[16,8192]{1,0:T(8,128)S(1)} %collective-permute-done.1.next_ref), custom_call_target="tpu_custom_call" | custom-call | tf_op jit(solution)/shard_map/pallas_call | solution.py:318
  51.2 4.8 %collective-permute-start.2 = (f32[2,16,8192]{2,1,0:T(8,128)}, f32[2,16,8192]{2,1,0:T(8,128)S(1)}, u32[]{:S(2)}, u32[]{:S(2)}) collective-permute-start(f32[2,16,8192]{2,1,0:T(8,128)} %shard_map.87.near_hbm), channel_id=1, source_target_pairs={{0,2},{1,3},{2,0},{3,1},{4,6},{5,7},{6,4},{7,5},{8,10},{9,11},{10,... | collective-permute-start | bytes 3145736 | tf_op jit(solution)/shard_map/ppermute | solution.py:338
  56.1 5.1 %all-to-all-done.2.recv_ref = f32[16,16,128]{2,1,0:T(8,128)S(1)} async-done(((f32[16,16,128]{2,1,0:T(8,128)}), f32[16,16,128]{2,1,0:T(8,128)S(1)}, u32[]{:S(2)}, u32[]{:S(2)}) %all-to-all-start.2) | async-done | bytes 131104 | tf_op jit(solution)/shard_map/all_to_all | solution.py:324
  61.2 10.0 %all_to_all.25.own_ref = f32[4,288,128]{2,1,0:T(8,128)S(1)} all-to-all(f32[4,288,128]{2,1,0:T(8,128)S(1)} %shard_map.86), channel_id=1, replica_groups=mesh['z'=16,'x'=4,'core'=2,'y'=4] {'x'}, dimensions={0} | all-to-all | bytes 1179648 | tf_op jit(solution)/shard_map/all_to_all | solution.py:324
  71.2 6.7 %collective-permute-start = (f32[4,288,128]{2,1,0:T(8,128)S(1)}, f32[4,288,128]{2,1,0:T(8,128)S(1)}, u32[]{:S(2)}, u32[]{:S(2)}) collective-permute-start(f32[4,288,128]{2,1,0:T(8,128)S(1)} %all_to_all.25.own_ref), channel_id=1, source_target_pairs={{0,4},{4,0},{1,5},{5,1},{2,6},{6,2},{3,7},{7,3},{8,12},{12,8},{9,1... | collective-permute-start | bytes 1769480 | tf_op jit(solution)/shard_map/ppermute | solution.py:372
  78.4 1.0 copy-done
  79.4 2.8 %shard_map.88.inv_ref = bf16[8192,128]{1,0:T(8,128)(2,1)S(1)} custom-call(f32[2,16,8192]{2,1,0:T(8,128)} %shard_map.87.near_hbm, f32[2,16,8192]{2,1,0:T(8,128)} %copy-done), custom_call_target="tpu_custom_call" | custom-call | flops 10485760 | bytes 4194304 | tf_op jit(solution)/shard_map/pallas_call | solution.py:318
  82.2 1.2 shard_map.89
  83.4 1.8 %shard_map.90 = (f32[16,8448]{1,0:T(8,128)S(1)}, f32[2,8448]{1,0:T(2,128)S(1)}, f32[64,8,128]{2,1,0:T(8,128)S(1)}) custom-call(s32[128]{0:T(128)S(1)} %convert_element_type.6.base_ref, s32[128]{0:T(128)S(1)} %convert_element_type.7.count_ref, f32[4,288,128]{2,1,0:T(8,128)S(1)} %collective-permute-done.other_ref, ...), custom_call_target="tpu_custom_call", output_to_operand_aliasing={{0}: (4, {}), {1}: (5, {})} | custom-call | flops 67108864 | bytes 2097152 | tf_op jit(solution)/shard_map/pallas_call | solution.py:318
  85.2 30.2 %all_to_all.26.pieces_ref = f32[64,8,128]{2,1,0:T(8,128)S(1)} all-to-all(f32[64,8,128]{2,1,0:T(8,128)S(1)} %get-tuple-element.34), channel_id=1, replica_groups=mesh['z'=16,'x'=4,'core'=2,'y'=4] {'z','x'}, dimensions={0} | all-to-all | bytes 524288 | tf_op jit(solution)/shard_map/all_to_all | solution.py:324
  115.4 8.0 %collective-permute-start.3 = (f32[64,8,128]{2,1,0:T(8,128)S(1)}, f32[64,8,128]{2,1,0:T(8,128)S(1)}, u32[]{:S(2)}, u32[]{:S(2)}) collective-permute-start(f32[64,8,128]{2,1,0:T(8,128)S(1)} %all_to_all.26.pieces_ref), channel_id=1, source_target_pairs={{0,4},{4,0},{1,5},{5,1},{2,6},{6,2},{3,7},{7,3},{8,12},{12,8},{9,1... | collective-permute-start | bytes 786440 | tf_op jit(solution)/shard_map/ppermute | solution.py:395
  123.4 9.1 %shard_map.91 = (bf16[3072,512]{1,0:T(8,128)(2,1)S(1)}, bf16[1024,512]{1,0:T(8,128)(2,1)}, bf16[4096,512]{1,0:T(8,128)(2,1)}) custom-call(f32[2,8448]{1,0:T(2,128)S(1)} %get-tuple-element.35.obs_ref, f32[2,256]{1,0:T(2,128)S(1)} %get-tuple-element.36.xy_ref), custom_call_target="tpu_custom_call" | custom-call | flops 41943040 | bytes 8388608 | tf_op jit(solution)/shard_map/pallas_call | solution.py:318
  132.5 2.8 %shard_map.92 = (f32[16,256]{1,0:T(8,128)S(1)}, bf16[4096,512]{1,0:T(8,128)(2,1)S(1)}) custom-call(f32[64,8,128]{2,1,0:T(8,128)S(1)} %all_to_all.26.pieces_ref, bf16[3072,512]{1,0:T(8,128)(2,1)S(1)} %get-tuple-element.37.kept_ref, bf16[1024,512]{1,0:T(8,128)(2,1)} %get-tuple-element.38.own_hbm, bf16[4096,512]{1,0:T(8,128)(2,1)} %get-tuple-element.39.other_hbm), custom_call_target="tpu_custom_call" | custom-call | flops 134217728 | bytes 8388608 | tf_op jit(solution)/shard_map/pallas_call | solution.py:318
  135.3 1.4 %shard_map.93 = f32[16,256]{1,0:T(8,128)} custom-call(f32[64,8,128]{2,1,0:T(8,128)S(1)} %collective-permute-done.3.pieces_ref, bf16[4096,512]{1,0:T(8,128)(2,1)S(1)} %get-tuple-element.40.tile_ref, f32[16,256]{1,0:T(8,128)S(1)} %get-tuple-element.41.partial_ref, f32[16,256]{1,0:T(8,128)S(1)} %get-tuple-element.42.field_ref), custom_call_target="tpu_custom_call" | custom-call | flops 134217728 | bytes 4194304 | tf_op jit(solution)/shard_map/pallas_call | solution.py:318
  (11 shorter events, 0.5 us)
Async XLA Ops:
  2.5 16.6 %all-to-all-start = ((f32[8,16,512]{2,1,0:T(8,128)}), f32[8,16,512]{2,1,0:T(8,128)S(1)}, u32[]{:S(2)}, u32[]{:S(2)}) async-start(f32[8,16,512]{2,1,0:T(8,128)} %shard_map.82), calls=%async_computation | async-start | bytes 524288 | tf_op jit(solution)/shard_map/all_to_all | solution.py:324
  19.9 22.5 %all-to-all-start.1 = ((f32[16,16,128]{2,1,0:T(8,128)}), f32[16,16,128]{2,1,0:T(8,128)S(1)}, u32[]{:S(2)}, u32[]{:S(2)}) async-start(f32[16,16,128]{2,1,0:T(8,128)} %get-tuple-element.25), calls=%async_computation.1 | async-start | bytes 262144 | tf_op jit(solution)/shard_map/all_to_all | solution.py:324
  30.5 18.7 %collective-permute-start.1 = (f32[16,8192]{1,0:T(8,128)}, f32[16,8192]{1,0:T(8,128)S(1)}, u32[]{:S(2)}, u32[]{:S(2)}) collective-permute-start(f32[16,8192]{1,0:T(8,128)} %own_hbm.1), channel_id=1, source_target_pairs={{0,1},{1,0},{2,3},{3,2},{4,5},{5,4},{6,7},{7,6},{8,9},{9,8},{10,11... | collective-permute-start | bytes 1572872 | tf_op jit(solution)/shard_map/ppermute | solution.py:329
  43.5 17.7 %all-to-all-start.2 = ((f32[16,16,128]{2,1,0:T(8,128)}), f32[16,16,128]{2,1,0:T(8,128)S(1)}, u32[]{:S(2)}, u32[]{:S(2)}) async-start(f32[16,16,128]{2,1,0:T(8,128)} %get-tuple-element.31), calls=%async_computation.2 | async-start | bytes 262144 | tf_op jit(solution)/shard_map/all_to_all | solution.py:324
  51.2 27.1 %collective-permute-start.2 = (f32[2,16,8192]{2,1,0:T(8,128)}, f32[2,16,8192]{2,1,0:T(8,128)S(1)}, u32[]{:S(2)}, u32[]{:S(2)}) collective-permute-start(f32[2,16,8192]{2,1,0:T(8,128)} %shard_map.87.near_hbm), channel_id=1, source_target_pairs={{0,2},{1,3},{2,0},{3,1},{4,6},{5,7},{6,4},{7,5},{8,10},{9,11},{10,... | collective-permute-start | bytes 3145736 | tf_op jit(solution)/shard_map/ppermute | solution.py:338
  71.2 12.2 %collective-permute-start = (f32[4,288,128]{2,1,0:T(8,128)S(1)}, f32[4,288,128]{2,1,0:T(8,128)S(1)}, u32[]{:S(2)}, u32[]{:S(2)}) collective-permute-start(f32[4,288,128]{2,1,0:T(8,128)S(1)} %all_to_all.25.own_ref), channel_id=1, source_target_pairs={{0,4},{4,0},{1,5},{5,1},{2,6},{6,2},{3,7},{7,3},{8,12},{12,8},{9,1... | collective-permute-start | bytes 1769480 | tf_op jit(solution)/shard_map/ppermute | solution.py:372
  78.3 1.0 copy-start
  115.4 19.9 %collective-permute-start.3 = (f32[64,8,128]{2,1,0:T(8,128)S(1)}, f32[64,8,128]{2,1,0:T(8,128)S(1)}, u32[]{:S(2)}, u32[]{:S(2)}) collective-permute-start(f32[64,8,128]{2,1,0:T(8,128)S(1)} %all_to_all.26.pieces_ref), channel_id=1, source_target_pairs={{0,4},{4,0},{1,5},{5,1},{2,6},{6,2},{3,7},{7,3},{8,12},{12,8},{9,1... | collective-permute-start | bytes 786440 | tf_op jit(solution)/shard_map/ppermute | solution.py:395

commit v5 on v4

--- a/solution.py
+++ b/solution.py
@@ -256,6 +256,9 @@
             copy.wait()
 
 
+AHEAD = 8
+
+
 def coef_chunk(pieces_ref, k):
     lane = lax.broadcasted_iota(jnp.int32, (S // 2, CAP), 1)
     blocks = []
@@ -267,37 +270,42 @@
     return jnp.concatenate(split2(jnp.concatenate(blocks, axis=1)), axis=0)
 
 
-def fold(acc):
+def chunk_copies(tile_hbm, chunks, ref, sems):
+    copies = [
+        pltpu.make_async_copy(tile_hbm.at[pl.ds(k * CHUNK, CHUNK)], ref.at[pl.ds(i * CHUNK, CHUNK)], sems.at[i])
+        for i, k in enumerate(chunks)
+    ]
+    for copy in copies:
+        copy.start()
+    return copies
+
+
+def half_product(pieces_ref, kept_ref, buf, copies):
+    kept = HALF // CHUNK - len(copies)
+    acc = jnp.zeros((2 * S, 2 * NB), F32)
+    for k in range(HALF // CHUNK):
+        left = coef_chunk(pieces_ref, k)
+        if k < kept:
+            right = kept_ref[k * CHUNK : (k + 1) * CHUNK]
+        else:
+            copies[k - kept].wait()
+            right = buf[(k - kept) * CHUNK : (k - kept + 1) * CHUNK]
+        acc = acc + dot(left, right)
     acc = acc[:S] + acc[S:]
     return acc[:, :NB] + acc[:, NB:]
 
 
-def own_half_kernel(pieces_ref, kept_ref, own_hbm, other_hbm, out_ref, other_ref, buf, sems, other_sem):
-    steps = HALF // CHUNK
-    rows = [pl.ds(i * CHUNK, CHUNK) for i in range(steps)]
-    copies = [pltpu.make_async_copy(own_hbm.at[rows[i]], buf.at[i], sems.at[i]) for i in range(steps - KEPT)]
-    others = [pltpu.make_async_copy(other_hbm.at[rows[i]], other_ref.at[rows[i]], other_sem.at[i]) for i in range(steps)]
-    for copy in copies + others:
-        copy.start()
-    acc = jnp.zeros((2 * S, 2 * NB), F32)
-    for k in range(steps):
-        left = coef_chunk(pieces_ref, k)
-        if k < KEPT:
-            right = kept_ref[rows[k]]
-        else:
-            copies[k - KEPT].wait()
-            right = buf[k - KEPT]
-        acc = acc + dot(left, right)
-    out_ref[...] = fold(acc)
-    for copy in others:
+def own_half_kernel(pieces_ref, kept_ref, own_hbm, other_hbm, out_ref, ahead_ref, buf, sems, ahead_sems):
+    copies = chunk_copies(own_hbm, range(HALF // CHUNK - KEPT), buf, sems)
+    ahead = chunk_copies(other_hbm, range(AHEAD), ahead_ref, ahead_sems)
+    out_ref[...] = half_product(pieces_ref, kept_ref, buf, copies)
+    for copy in ahead:
         copy.wait()
 
 
-def other_half_kernel(pieces_ref, tile_ref, partial_ref, field_ref, out_ref):
-    acc = jnp.zeros((2 * S, 2 * NB), F32)
-    for k in range(HALF // CHUNK):
-        acc = acc + dot(coef_chunk(pieces_ref, k), tile_ref[k * CHUNK : (k + 1) * CHUNK])
-    out_ref[...] = field_ref[...] + (partial_ref[...] + fold(acc))
+def other_half_kernel(pieces_ref, ahead_ref, other_hbm, partial_ref, field_ref, out_ref, buf, sems):
+    copies = chunk_copies(other_hbm, range(AHEAD, HALF // CHUNK), buf, sems)
+    out_ref[...] = field_ref[...] + (partial_ref[...] + half_product(pieces_ref, ahead_ref, buf, copies))
 
 
 def call(name, kernel, out, specs, scratch=(), flops=0, nbytes=0, out_specs=None, aliases=None):
@@ -393,23 +401,29 @@
     )(obs_xy, xy)
     own = exchange(piece, ("z", "x"))
     other = lax.ppermute(own, "core", [(0, 1), (1, 0)])
-    streamed = HALF // CHUNK - KEPT
-    partial, other_tile = call(
+    streamed, late = HALF // CHUNK - KEPT, HALF // CHUNK - AHEAD
+    partial, ahead = call(
         "own_half",
         own_half_kernel,
-        [((S, NB), F32), ((HALF, 2 * NB), BF16)],
+        [((S, NB), F32), ((AHEAD * CHUNK, 2 * NB), BF16)],
         [VMEM, VMEM, HBM, HBM],
         [
-            pltpu.VMEM((streamed, CHUNK, 2 * NB), BF16),
+            pltpu.VMEM((streamed * CHUNK, 2 * NB), BF16),
             pltpu.SemaphoreType.DMA((streamed,)),
-            pltpu.SemaphoreType.DMA((HALF // CHUNK,)),
+            pltpu.SemaphoreType.DMA((AHEAD,)),
         ],
         flops=2 * 2 * S * NB * M,
         nbytes=4 * NB * M,
     )(own, kept, own_tile, other_tile)
-    return call("other_half", other_half_kernel, [((S, NB), F32)], [VMEM] * 4, flops=2 * 2 * S * NB * M, nbytes=2 * NB * M)(
-        other, other_tile, partial, field
-    )[0]
+    return call(
+        "other_half",
+        other_half_kernel,
+        [((S, NB), F32)],
+        [VMEM, VMEM, HBM, VMEM, VMEM],
+        [pltpu.VMEM((late * CHUNK, 2 * NB), BF16), pltpu.SemaphoreType.DMA((late,))],
+        flops=2 * 2 * S * NB * M,
+        nbytes=2 * NB * M,
+    )(other, ahead, other_tile, partial, field)[0]
 
 
 def solution(mesh):

time: 137 us -> 138 us (level)
  transfers between devices with their start and end apart: 7 -> 7, of which waited for: 3 -> 3; matrix products, arithmetic and copies ran while one was open for 0% -> 0% of each run, Pallas kernels for 15% -> 14%
where the time goes in v5:
time: 138 us; the launch traced here: 137 us
  starting transfers between devices  49.1 us (36%)
  blocking collectives  40.1 us (29%)
  Pallas kernels  26.8 us (19%)
  waiting for transfers between devices  19 us (14%)
    all_to_all x2, blocking collectives, exchange(): return lax.all_to_all(piece, axes, 0, 0, tiled=True)  40.1 us
    pallas_call x12, Pallas kernels, run(): made(*(pltpu.with_memory_space_constraint(a, pltpu.MemorySpace.HBM) if sp...  26.8 us
    all_to_all x3, starting transfers between devices, exchange(): return lax.all_to_all(piece, axes, 0, 0, tiled=True)  26.4 us
    all_to_all x3, waiting for transfers between devices, exchange(): return lax.all_to_all(piece, axes, 0, 0, tiled=True)  19 us
    ppermute x2, starting transfers between devices, body(): other = lax.ppermute(own, 'core', [(0, 1), (1, 0)])  14.7 us
    ppermute x1, starting transfers between devices, body(): far_pair = lax.ppermute(pair, 'y', [(y, y ^ 2) for y in range(4)])  4.82 us
    ppermute x1, starting transfers between devices, body(): block = lax.ppermute(inverse_rows, 'y', [(y, y ^ 1) for y in range(4)])  3.21 us
  transfers between devices with their start and end apart: 7, of which 3 were waited for; matrix products, arithmetic and copies ran while one was open for 0% of the time, Pallas kernels for 14%

profile of v5, /device:TPU:1, one launch (start us, length us, event | category | flops | bytes accessed | tf_op | source)
XLA Modules:
  0.0 137.2 jit_solution(3583865388581383584)
XLA Ops:
  0.7 1.9 %shard_map.82 = f32[8,16,512]{2,1,0:T(8,128)} custom-call(bf16[16,256]{1,0:T(8,128)(2,1)} %z_hbm.1, bf16[448,256]{1,0:T(8,128)(2,1)} %bitcast.3, s32[1]{0:T(128)S(6)} %copy.13.count_ref), custom_call_target="tpu_custom_call" | custom-call | tf_op jit(solution)/shard_map/pallas_call | solution.py:326
  2.5 10.2 %all-to-all-start = ((f32[8,16,512]{2,1,0:T(8,128)}), f32[8,16,512]{2,1,0:T(8,128)S(1)}, u32[]{:S(2)}, u32[]{:S(2)}) async-start(f32[8,16,512]{2,1,0:T(8,128)} %shard_map.82), calls=%async_computation | async-start | bytes 524288 | tf_op jit(solution)/shard_map/all_to_all | solution.py:332
  12.7 1.3 shard_map.83
  14.0 5.2 %all-to-all-done.recv_ref = f32[8,16,512]{2,1,0:T(8,128)S(1)} async-done(((f32[8,16,512]{2,1,0:T(8,128)}), f32[8,16,512]{2,1,0:T(8,128)S(1)}, u32[]{:S(2)}, u32[]{:S(2)}) %all-to-all-start) | async-done | bytes 262176 | tf_op jit(solution)/shard_map/all_to_all | solution.py:332
  19.2 0.8 shard_map.84
  19.9 10.5 %all-to-all-start.1 = ((f32[16,16,128]{2,1,0:T(8,128)}), f32[16,16,128]{2,1,0:T(8,128)S(1)}, u32[]{:S(2)}, u32[]{:S(2)}) async-start(f32[16,16,128]{2,1,0:T(8,128)} %get-tuple-element.25), calls=%async_computation.1 | async-start | bytes 262144 | tf_op jit(solution)/shard_map/all_to_all | solution.py:332
  30.5 3.2 %collective-permute-start.1 = (f32[16,8192]{1,0:T(8,128)}, f32[16,8192]{1,0:T(8,128)S(1)}, u32[]{:S(2)}, u32[]{:S(2)}) collective-permute-start(f32[16,8192]{1,0:T(8,128)} %own_hbm.1), channel_id=1, source_target_pairs={{0,1},{1,0},{2,3},{3,2},{4,5},{5,4},{6,7},{7,6},{8,9},{9,8},{10,11... | collective-permute-start | bytes 1572872 | tf_op jit(solution)/shard_map/ppermute | solution.py:337
  33.7 8.7 %all-to-all-done.1.recv_ref.extra_ref = f32[16,16,128]{2,1,0:T(8,128)S(1)} async-done(((f32[16,16,128]{2,1,0:T(8,128)}), f32[16,16,128]{2,1,0:T(8,128)S(1)}, u32[]{:S(2)}, u32[]{:S(2)}) %all-to-all-start.1) | async-done | bytes 131104 | tf_op jit(solution)/shard_map/all_to_all | solution.py:332
  42.4 1.0 shard_map.85
  43.5 5.7 %all-to-all-start.2 = ((f32[16,16,128]{2,1,0:T(8,128)}), f32[16,16,128]{2,1,0:T(8,128)S(1)}, u32[]{:S(2)}, u32[]{:S(2)}) async-start(f32[16,16,128]{2,1,0:T(8,128)} %get-tuple-element.31), calls=%async_computation.2 | async-start | bytes 262144 | tf_op jit(solution)/shard_map/all_to_all | solution.py:332
  49.2 2.1 %shard_map.87.near_hbm = f32[2,16,8192]{2,1,0:T(8,128)} custom-call(f32[16,8192]{1,0:T(8,128)} %own_hbm.1, f32[16,8192]{1,0:T(8,128)S(1)} %collective-permute-done.1.next_ref), custom_call_target="tpu_custom_call" | custom-call | tf_op jit(solution)/shard_map/pallas_call | solution.py:326
  51.2 4.8 %collective-permute-start.2 = (f32[2,16,8192]{2,1,0:T(8,128)}, f32[2,16,8192]{2,1,0:T(8,128)S(1)}, u32[]{:S(2)}, u32[]{:S(2)}) collective-permute-start(f32[2,16,8192]{2,1,0:T(8,128)} %shard_map.87.near_hbm), channel_id=1, source_target_pairs={{0,2},{1,3},{2,0},{3,1},{4,6},{5,7},{6,4},{7,5},{8,10},{9,11},{10,... | collective-permute-start | bytes 3145736 | tf_op jit(solution)/shard_map/ppermute | solution.py:346
  56.1 5.1 %all-to-all-done.2.recv_ref = f32[16,16,128]{2,1,0:T(8,128)S(1)} async-done(((f32[16,16,128]{2,1,0:T(8,128)}), f32[16,16,128]{2,1,0:T(8,128)S(1)}, u32[]{:S(2)}, u32[]{:S(2)}) %all-to-all-start.2) | async-done | bytes 131104 | tf_op jit(solution)/shard_map/all_to_all | solution.py:332
  61.2 10.0 %all_to_all.25.own_ref = f32[4,288,128]{2,1,0:T(8,128)S(1)} all-to-all(f32[4,288,128]{2,1,0:T(8,128)S(1)} %shard_map.86), channel_id=1, replica_groups=mesh['z'=16,'x'=4,'core'=2,'y'=4] {'x'}, dimensions={0} | all-to-all | bytes 1179648 | tf_op jit(solution)/shard_map/all_to_all | solution.py:332
  71.2 6.7 %collective-permute-start = (f32[4,288,128]{2,1,0:T(8,128)S(1)}, f32[4,288,128]{2,1,0:T(8,128)S(1)}, u32[]{:S(2)}, u32[]{:S(2)}) collective-permute-start(f32[4,288,128]{2,1,0:T(8,128)S(1)} %all_to_all.25.own_ref), channel_id=1, source_target_pairs={{0,4},{4,0},{1,5},{5,1},{2,6},{6,2},{3,7},{7,3},{8,12},{12,8},{9,1... | collective-permute-start | bytes 1769480 | tf_op jit(solution)/shard_map/ppermute | solution.py:380
  78.4 1.0 copy-done
  79.4 2.8 %shard_map.88.inv_ref = bf16[8192,128]{1,0:T(8,128)(2,1)S(1)} custom-call(f32[2,16,8192]{2,1,0:T(8,128)} %shard_map.87.near_hbm, f32[2,16,8192]{2,1,0:T(8,128)} %copy-done), custom_call_target="tpu_custom_call" | custom-call | flops 10485760 | bytes 4194304 | tf_op jit(solution)/shard_map/pallas_call | solution.py:326
  82.2 1.2 shard_map.89
  83.4 1.8 %shard_map.90 = (f32[16,8448]{1,0:T(8,128)S(1)}, f32[2,8448]{1,0:T(2,128)S(1)}, f32[64,8,128]{2,1,0:T(8,128)S(1)}) custom-call(s32[128]{0:T(128)S(1)} %convert_element_type.6.base_ref, s32[128]{0:T(128)S(1)} %convert_element_type.7.count_ref, f32[4,288,128]{2,1,0:T(8,128)S(1)} %collective-permute-done.other_ref, ...), custom_call_target="tpu_custom_call", output_to_operand_aliasing={{0}: (4, {}), {1}: (5, {})} | custom-call | flops 67108864 | bytes 2097152 | tf_op jit(solution)/shard_map/pallas_call | solution.py:326
  85.2 30.2 %all_to_all.26.pieces_ref = f32[64,8,128]{2,1,0:T(8,128)S(1)} all-to-all(f32[64,8,128]{2,1,0:T(8,128)S(1)} %get-tuple-element.34), channel_id=1, replica_groups=mesh['z'=16,'x'=4,'core'=2,'y'=4] {'z','x'}, dimensions={0} | all-to-all | bytes 524288 | tf_op jit(solution)/shard_map/all_to_all | solution.py:332
  115.4 8.0 %collective-permute-start.3 = (f32[64,8,128]{2,1,0:T(8,128)S(1)}, f32[64,8,128]{2,1,0:T(8,128)S(1)}, u32[]{:S(2)}, u32[]{:S(2)}) collective-permute-start(f32[64,8,128]{2,1,0:T(8,128)S(1)} %all_to_all.26.pieces_ref), channel_id=1, source_target_pairs={{0,4},{4,0},{1,5},{5,1},{2,6},{6,2},{3,7},{7,3},{8,12},{12,8},{9,1... | collective-permute-start | bytes 786440 | tf_op jit(solution)/shard_map/ppermute | solution.py:403
  123.4 9.1 %shard_map.91 = (bf16[3072,512]{1,0:T(8,128)(2,1)S(1)}, bf16[1024,512]{1,0:T(8,128)(2,1)}, bf16[4096,512]{1,0:T(8,128)(2,1)}) custom-call(f32[2,8448]{1,0:T(2,128)S(1)} %get-tuple-element.35.obs_ref, f32[2,256]{1,0:T(2,128)S(1)} %get-tuple-element.36.xy_ref), custom_call_target="tpu_custom_call" | custom-call | flops 41943040 | bytes 8388608 | tf_op jit(solution)/shard_map/pallas_call | solution.py:326
  132.5 2.1 %shard_map.92 = (f32[16,256]{1,0:T(8,128)S(1)}, bf16[2048,512]{1,0:T(8,128)(2,1)S(1)}) custom-call(f32[64,8,128]{2,1,0:T(8,128)S(1)} %all_to_all.26.pieces_ref, bf16[3072,512]{1,0:T(8,128)(2,1)S(1)} %get-tuple-element.37.kept_ref, bf16[1024,512]{1,0:T(8,128)(2,1)} %get-tuple-element.38.own_hbm, bf16[4096,512]{1,0:T(8,128)(2,1)} %get-tuple-element.39.other_hbm), custom_call_target="tpu_custom_call" | custom-call | flops 134217728 | bytes 8388608 | tf_op jit(solution)/shard_map/pallas_call | solution.py:326
  134.6 2.6 %shard_map.93 = f32[16,256]{1,0:T(8,128)} custom-call(f32[64,8,128]{2,1,0:T(8,128)S(1)} %collective-permute-done.3.pieces_ref, bf16[2048,512]{1,0:T(8,128)(2,1)S(1)} %get-tuple-element.40.ahead_ref, bf16[4096,512]{1,0:T(8,128)(2,1)} %get-tuple-element.39.other_hbm, f32[16,256]{1,0:T(8,128)S(1)} %get-tuple-element.41.partial_ref, ...), custom_call_target="tpu_custom_call" | custom-call | flops 134217728 | bytes 4194304 | tf_op jit(solution)/shard_map/pallas_call | solution.py:326
  (11 shorter events, 0.5 us)
Async XLA Ops:
  2.5 16.6 %all-to-all-start = ((f32[8,16,512]{2,1,0:T(8,128)}), f32[8,16,512]{2,1,0:T(8,128)S(1)}, u32[]{:S(2)}, u32[]{:S(2)}) async-start(f32[8,16,512]{2,1,0:T(8,128)} %shard_map.82), calls=%async_computation | async-start | bytes 524288 | tf_op jit(solution)/shard_map/all_to_all | solution.py:332
  19.9 22.5 %all-to-all-start.1 = ((f32[16,16,128]{2,1,0:T(8,128)}), f32[16,16,128]{2,1,0:T(8,128)S(1)}, u32[]{:S(2)}, u32[]{:S(2)}) async-start(f32[16,16,128]{2,1,0:T(8,128)} %get-tuple-element.25), calls=%async_computation.1 | async-start | bytes 262144 | tf_op jit(solution)/shard_map/all_to_all | solution.py:332
  30.5 18.7 %collective-permute-start.1 = (f32[16,8192]{1,0:T(8,128)}, f32[16,8192]{1,0:T(8,128)S(1)}, u32[]{:S(2)}, u32[]{:S(2)}) collective-permute-start(f32[16,8192]{1,0:T(8,128)} %own_hbm.1), channel_id=1, source_target_pairs={{0,1},{1,0},{2,3},{3,2},{4,5},{5,4},{6,7},{7,6},{8,9},{9,8},{10,11... | collective-permute-start | bytes 1572872 | tf_op jit(solution)/shard_map/ppermute | solution.py:337
  43.5 17.7 %all-to-all-start.2 = ((f32[16,16,128]{2,1,0:T(8,128)}), f32[16,16,128]{2,1,0:T(8,128)S(1)}, u32[]{:S(2)}, u32[]{:S(2)}) async-start(f32[16,16,128]{2,1,0:T(8,128)} %get-tuple-element.31), calls=%async_computation.2 | async-start | bytes 262144 | tf_op jit(solution)/shard_map/all_to_all | solution.py:332
  51.2 27.1 %collective-permute-start.2 = (f32[2,16,8192]{2,1,0:T(8,128)}, f32[2,16,8192]{2,1,0:T(8,128)S(1)}, u32[]{:S(2)}, u32[]{:S(2)}) collective-permute-start(f32[2,16,8192]{2,1,0:T(8,128)} %shard_map.87.near_hbm), channel_id=1, source_target_pairs={{0,2},{1,3},{2,0},{3,1},{4,6},{5,7},{6,4},{7,5},{8,10},{9,11},{10,... | collective-permute-start | bytes 3145736 | tf_op jit(solution)/shard_map/ppermute | solution.py:346
  71.2 12.2 %collective-permute-start = (f32[4,288,128]{2,1,0:T(8,128)S(1)}, f32[4,288,128]{2,1,0:T(8,128)S(1)}, u32[]{:S(2)}, u32[]{:S(2)}) collective-permute-start(f32[4,288,128]{2,1,0:T(8,128)S(1)} %all_to_all.25.own_ref), channel_id=1, source_target_pairs={{0,4},{4,0},{1,5},{5,1},{2,6},{6,2},{3,7},{7,3},{8,12},{12,8},{9,1... | collective-permute-start | bytes 1769480 | tf_op jit(solution)/shard_map/ppermute | solution.py:380
  78.3 1.0 copy-start
  115.4 19.2 %collective-permute-start.3 = (f32[64,8,128]{2,1,0:T(8,128)S(1)}, f32[64,8,128]{2,1,0:T(8,128)S(1)}, u32[]{:S(2)}, u32[]{:S(2)}) collective-permute-start(f32[64,8,128]{2,1,0:T(8,128)S(1)} %all_to_all.26.pieces_ref), channel_id=1, source_target_pairs={{0,4},{4,0},{1,5},{5,1},{2,6},{6,2},{3,7},{7,3},{8,12},{12,8},{9,1... | collective-permute-start | bytes 786440 | tf_op jit(solution)/shard_map/ppermute | solution.py:403
